TPU v7x, 512 devices: a whole 4x8x8 slice. The times are simulated.
512 devices in a mesh: dp: 64 (over y, z), blk: 8 (over x, core).
Axes of the slice: x: 4, y: 8, z: 8, core: 2. Of those that a mesh axis runs over, the one named last changes fastest.
Arguments:
- queries: bfloat16 [8, 256, 32, 128], P('blk', 'dp'), may hold values from -6 to 6
- passages: bfloat16 [8, 1024, 192, 128], P('blk', 'dp'), may hold values from -6 to 6
- passage_lengths: int32 [8, 1024], P('blk', 'dp'), may hold values from 32 to 192
- positives: bfloat16 [8, 256, 192, 128], P('blk', 'dp'), may hold values from -6 to 6
- positive_lengths: int32 [8, 256], P('blk', 'dp'), may hold values from 32 to 192
- owners: int32 [8, 256, 32, 1], P('blk', 'dp'), may hold values from 0 to 63; in each aligned block of 128 rows (0 to 127, 128 to 255, ..., all dimensions but the last counted through in order) at most 4 rows name the same one
- local_ids: int32 [8, 256, 32], P('blk', 'dp'), may hold values from 0 to 15
- teacher: float32 [8, 256, 32], P('blk', 'dp'), may hold values from -12 to 12
Outputs:
- student: float32 [8, 256, 32], P('blk', 'dp')
- distill: float32 [8, 256], P('blk', 'dp')
- contrast: float32 [8, 256], P('blk', 'dp')
Inputs may be any that keep to these rules, and one draw needn't show every extreme that they name: `owners`: among the 128 candidate pairs of the queries of one device, no owner is named more than 4 times, a bound that some block reaches.
All inputs are finite; a program needn't handle non-finite values.
Results may differ from a plain program's by a relative error of at most 0.00062.
Values may be sent and summed in bfloat16 or wider, within the bound.
A program may use at most 64 MiB of HBM per device.

v0:
```python
import math

import jax
import jax.numpy as jnp
from jax import lax
from jax.sharding import PartitionSpec as P


def unit_rows(values):
    wide = values.astype(jnp.float32)
    total = jnp.sum(wide * wide, axis=-1, keepdims=True) + 1e-06
    return (wide * lax.rsqrt(total)).astype(jnp.bfloat16)


def slot_ranks(destination, peer_count):
    onehot = (destination[:, None] == jnp.arange(peer_count, dtype=jnp.int32)[None, :]).astype(
        jnp.int32
    )
    before = jnp.cumsum(onehot, axis=0) - onehot
    return jnp.sum(before * onehot, axis=1)


def slot_scores(slot_queries, slot_ids, passage_unit, kept_lengths):
    row_count = slot_queries.shape[0]
    block_rows = math.gcd(row_count, 64)
    query_blocks = slot_queries.reshape(
        row_count // block_rows, block_rows, slot_queries.shape[1], slot_queries.shape[2]
    )
    id_blocks = slot_ids.reshape(row_count // block_rows, block_rows)

    def slot_block_relevance(inputs):
        query_tile_rows, id_block = inputs
        document_rows = passage_unit[id_block]
        similarity_matrix = jnp.einsum(
            "uhv,uyv->uhy", query_tile_rows, document_rows, preferred_element_type=jnp.float32
        )
        usable = (
            lax.broadcasted_iota(jnp.int32, (1, 1, document_rows.shape[1]), 2)
            < kept_lengths[id_block][:, None, None]
        )
        return jnp.sum(jnp.max(jnp.where(usable, similarity_matrix, -1000000000.0), axis=2), axis=1)

    return lax.map(slot_block_relevance, (query_blocks, id_blocks)).reshape(row_count)


def cross_scores(query_tile, document_rows, lengths):
    doc_count = document_rows.shape[0]
    block_docs = math.gcd(doc_count, 8)
    doc_blocks = document_rows.reshape(
        doc_count // block_docs, block_docs, document_rows.shape[1], document_rows.shape[2]
    )
    length_blocks = lengths.reshape(doc_count // block_docs, block_docs)

    def cross_block_relevance(inputs):
        document_tile_rows, length_block = inputs
        similarity_matrix = jnp.einsum(
            "aqd,kld->akql", query_tile, document_tile_rows, preferred_element_type=jnp.float32
        )
        usable = (
            lax.broadcasted_iota(jnp.int32, (1, 1, 1, document_tile_rows.shape[1]), 3)
            < length_block[None, :, None, None]
        )
        return jnp.sum(jnp.max(jnp.where(usable, similarity_matrix, -1000000000.0), axis=3), axis=2)

    scored = lax.map(cross_block_relevance, (doc_blocks, length_blocks))
    return jnp.moveaxis(scored, 0, 1).reshape(query_tile.shape[0], doc_count)


def send_back(scored):
    return lax.all_to_all(scored, "dp", split_axis=0, concat_axis=0, tiled=True)


def per_device(
    queries, passages, passage_lengths, positives, positive_lengths, owners, local_ids, teacher
):
    peer_count = lax.axis_size("dp")
    query_unit = unit_rows(queries[0])
    passage_unit = unit_rows(passages[0])
    kept_lengths = passage_lengths[0]
    query_count = query_unit.shape[0]
    cand_count = owners.shape[2]
    capacity = 2 * query_count * cand_count // peer_count
    destination = owners[0, :, :, 0].reshape(-1)
    passage_ids = local_ids[0].reshape(-1)
    slot_rank = slot_ranks(destination, peer_count)
    slot_index = destination * capacity + slot_rank
    pair_rows = query_unit[jnp.arange(destination.shape[0], dtype=jnp.int32) // cand_count]
    send_queries = (
        jnp.zeros((peer_count * capacity,) + query_unit.shape[1:], jnp.bfloat16)
        .at[slot_index]
        .set(pair_rows)
    )
    send_queries = send_queries.reshape((peer_count, capacity) + query_unit.shape[1:])
    send_ids = (
        jnp.zeros((peer_count * capacity,), jnp.int32)
        .at[slot_index]
        .set(passage_ids)
        .reshape(peer_count, capacity)
    )
    got_queries = lax.all_to_all(send_queries, "dp", split_axis=0, concat_axis=0, tiled=True)
    received_token_ids = lax.all_to_all(send_ids, "dp", split_axis=0, concat_axis=0, tiled=True)
    sources, items = received_token_ids.shape
    flat_queries = got_queries.reshape((sources * items,) + got_queries.shape[2:])
    scored = slot_scores(
        flat_queries, received_token_ids.reshape(-1), passage_unit, kept_lengths
    ).reshape(sources, items)
    returned = send_back(scored)
    student = returned.reshape(-1)[slot_index].reshape(query_count, cand_count)
    teacher_score_rows = teacher[0]
    log_teacher = teacher_score_rows - jnp.log(
        jnp.sum(jnp.exp(teacher_score_rows), axis=-1, keepdims=True)
    )
    log_student = student - jnp.log(jnp.sum(jnp.exp(student), axis=-1, keepdims=True))
    distill = jnp.sum(jnp.exp(log_teacher) * (log_teacher - log_student), axis=-1)
    positive_unit = unit_rows(positives[0])
    positive_kept = positive_lengths[0]
    doc_piece = lax.all_gather(positive_unit, "blk", axis=0, tiled=True)
    length_piece = lax.all_gather(positive_kept, "blk", axis=0, tiled=True)
    scored = cross_scores(query_unit, doc_piece, length_piece)
    own_column = lax.axis_index("blk") * query_count + jnp.arange(query_count, dtype=jnp.int32)
    own_logit = jnp.take_along_axis(scored, own_column[:, None], axis=1)[:, 0]
    contrast = jnp.log(jnp.sum(jnp.exp(scored), axis=-1)) - own_logit
    return (student[None], distill[None], contrast[None])


def solution(mesh):
    in_specs = (
        P("blk", "dp", None, None),
        P("blk", "dp", None, None),
        P("blk", "dp"),
        P("blk", "dp", None, None),
        P("blk", "dp"),
        P("blk", "dp", None, None),
        P("blk", "dp", None),
        P("blk", "dp", None),
    )
    out_specs = (P("blk", "dp", None), P("blk", "dp"), P("blk", "dp"))
    return jax.shard_map(
        per_device, mesh=mesh, in_specs=in_specs, out_specs=out_specs, check_vma=False
    )
```

profile of v0, /device:TPU:6, one launch (start us, length us, event | category | flops | bytes accessed | tf_op | source)
XLA Modules:
  0.0 182.6 jit_solution(7733625132189216451)
XLA Ops:
  7.2 1.1 fusion.12
  8.4 1.8 fusion.13
  10.2 0.5 broadcast.343
  10.7 1.3 fusion.23
  12.1 0.1 fusion.16
  12.2 0.8 reshape.344
  13.1 0.2 reduce_window_sum.11
  13.2 0.2 select_reduce_fusion.1
  13.4 1.0 scatter_custom_fusion
  14.4 0.7 all_to_all.15
  15.1 16.6 %all-to-all-start = ((s32[64,1,4]{2,1,0:T(1,128)}), s32[64,1,4]{2,1,0:T(1,128)S(1)}, u32[]{:S(2)}, u32[]{:S(2)}) async-start(s32[64,1,4]{2,1,0:T(1,128)} %bitcast.13), calls=%async_computation | async-start | bytes 65536 | tf_op jit(solution)/shard_map/all_to_all | solution.py:101
  31.7 1.3 dynamic-slice
  33.7 0.9 fusion.14
  34.5 0.8 bitcast_dynamic-update-slice_fusion.1
  35.3 0.8 fusion.15
  36.2 0.8 gather_fusion.2
  36.9 1.6 broadcast_in_dim.65
  38.6 13.7 %scatter_fusion = bf16[256,32,128]{2,1,0:T(8,128)(2,1)} fusion(bf16[256,32,128]{2,1,0:T(8,128)(2,1)} %broadcast_in_dim.65, s32[128]{0:T(128)S(1)} %fusion.20, bf16[128,32,128]{2,1,0:T(8,128)(2,1)S(1)} %gather_fusion.2), kind=kCustom, calls=%fused_computation.6 | custom fusion | bytes 3146240 | tf_op jit(solution)/shard_map/scatter | solution.py:91
  52.2 12.8 %all-to-all-start.1 = ((bf16[64,4,32,128]{3,2,1,0:T(8,128)(2,1)}), bf16[64,4,32,128]{3,2,1,0:T(8,128)(2,1)S(1)}, u32[]{:S(2)}, u32[]{:S(2)}) async-start(bf16[64,4,32,128]{3,2,1,0:T(8,128)(2,1)} %bitcast.18), calls=%async_computation.1 | async-start | bytes 4194304 | tf_op jit(solution)/shard_map/all_to_all | solution.py:100
  65.1 0.1 fusion.17
  65.2 7.3 %all-reduce = s32[32]{0:T(128)S(1)} all-reduce(s32[32]{0:T(128)S(1)} %bitcast_dynamic-update-slice_fusion.1), channel_id=2, replica_groups=mesh['dp'=64,'blk'=8] {'blk'}, use_global_device_ids=true, to_apply=%add | all-reduce | flops 32 | bytes 256
  72.5 0.1 reshape.294
  72.6 0.6 fusion.10
  73.3 1.6 fusion.11
  74.9 0.7 reduce.17
  75.6 0.1 reshape_reshape.7
  75.8 7.1 %while.21 = (s32[]{:T(128)}, f32[4,4,8]{2,1,0:T(4,128)S(1)}, s32[4,8]{1,0:T(4,128)S(1)}, bf16[4,8,192,128]{3,2,1,0:T(8,128)(2,1)}, bf16[4,32,128]{2,1,0:T(8,128)(2,1)S(1)}, /*index=5*/s32[]{:T(128)}, f32[]{:T(128)}) while((s32[]{:T(128)}, f32[4,4,8]{2,1,0:T(4,128)S(1)}, s32[4,8]{1,0:T(4,128)S(1)}, bf16[4,8,192,128]{3,2,1,0:T(8,128)(2,1)}, ...), condition=%wide.region_17.18_spmd, body=%wide.region_14.17_spmd.sunk | while | flops 50726368 | bytes 441925 | solution.py:65
  75.9 1.5 fusion.38
  77.6 1.5 fusion.38
  79.4 1.5 fusion.38
  81.2 1.5 fusion.38
  82.9 0.1 reshape.296
  82.9 0.7 gather_fusion.4
  83.6 0.1 exponential_reduce_fusion
  83.7 32.3 %all-to-all-done.1 = bf16[64,4,32,128]{3,2,1,0:T(8,128)(2,1)S(1)} async-done(((bf16[64,4,32,128]{3,2,1,0:T(8,128)(2,1)}), bf16[64,4,32,128]{3,2,1,0:T(8,128)(2,1)S(1)}, u32[]{:S(2)}, u32[]{:S(2)}) %all-to-all-start.1) | async-done | bytes 2097184 | tf_op jit(solution)/shard_map/all_to_all | solution.py:100
  116.0 30.9 %while.20 = (s32[]{:T(128)}, f32[4,64]{1,0:T(4,128)S(1)}, s32[4,64]{1,0:T(4,128)S(1)}, s32[16]{0:T(128)S(1)}, bf16[4,64,32,128]{3,2,1,0:T(8,128)(2,1)S(1)}, /*in...) while((s32[]{:T(128)}, f32[4,64]{1,0:T(4,128)S(1)}, s32[4,64]{1,0:T(4,128)S(1)}, ...), condition=%wide.region_9.10_spmd, body=%wide.region_6.9_spmd.sunk | while | flops 101463168 | bytes 10013557 | solution.py:43
  116.0 0.8 gather_fusion.1
  116.8 0.1 iota_compare_fusion.5
  116.9 2.6 %gather_fusion = bf16[64,192,128]{2,1,0:T(8,128)(2,1)} fusion(bf16[16,192,128]{2,1,0:T(8,128)(2,1)S(1)} %get-tuple-element.179, s32[1024]{0:T(1024)S(1)} %pad_clamp_fusion.4), kind=kCustom, calls=%fused_computation.1.clone.1 | custom fusion | bytes 6291712 | tf_op jit(solution)/shard_map/while/body/eval_jaxpr/gather | solution.py:33
  119.5 4.1 %select_reduce_fusion.3 = f32[64,32]{1,0:T(8,128)S(1)} fusion(bf16[64,192,128]{2,1,0:T(8,128)(2,1)} %gather_fusion, pred[64,192]{1,0:T(8,128)(4,1)S(1)} %iota_compare_fusion.5, bf16[4,64,32,128]{3,2,1,0:T(8,128)(2,1)S(1)} %get-tuple-element.178, s32[]{:T(128)S(6)} %copy.34), kind=kOutput, calls=%fused_computation.17.clone.1 | convolution fusion | flops 101447680 | bytes 3694596 | tf_op jit(solution)/shard_map/while/body/eval_jaxpr/uhv,uyv->uhy/dot_general | solution.py:34
  123.5 0.1 reduce_sum.113
  123.7 0.8 gather_fusion.1
  124.6 2.6 %gather_fusion = bf16[64,192,128]{2,1,0:T(8,128)(2,1)} fusion(bf16[16,192,128]{2,1,0:T(8,128)(2,1)S(1)} %get-tuple-element.179, s32[1024]{0:T(1024)S(1)} %pad_clamp_fusion.4), kind=kCustom, calls=%fused_computation.1.clone.1 | custom fusion | bytes 6291712 | tf_op jit(solution)/shard_map/while/body/eval_jaxpr/gather | solution.py:33
  127.2 4.1 %select_reduce_fusion.3 = f32[64,32]{1,0:T(8,128)S(1)} fusion(bf16[64,192,128]{2,1,0:T(8,128)(2,1)} %gather_fusion, pred[64,192]{1,0:T(8,128)(4,1)S(1)} %iota_compare_fusion.5, bf16[4,64,32,128]{3,2,1,0:T(8,128)(2,1)S(1)} %get-tuple-element.178, s32[]{:T(128)S(6)} %copy.34), kind=kOutput, calls=%fused_computation.17.clone.1 | convolution fusion | flops 101447680 | bytes 3694596 | tf_op jit(solution)/shard_map/while/body/eval_jaxpr/uhv,uyv->uhy/dot_general | solution.py:34
  131.3 0.1 reduce_sum.113
  131.5 0.8 gather_fusion.1
  132.3 2.6 %gather_fusion = bf16[64,192,128]{2,1,0:T(8,128)(2,1)} fusion(bf16[16,192,128]{2,1,0:T(8,128)(2,1)S(1)} %get-tuple-element.179, s32[1024]{0:T(1024)S(1)} %pad_clamp_fusion.4), kind=kCustom, calls=%fused_computation.1.clone.1 | custom fusion | bytes 6291712 | tf_op jit(solution)/shard_map/while/body/eval_jaxpr/gather | solution.py:33
  135.0 4.1 %select_reduce_fusion.3 = f32[64,32]{1,0:T(8,128)S(1)} fusion(bf16[64,192,128]{2,1,0:T(8,128)(2,1)} %gather_fusion, pred[64,192]{1,0:T(8,128)(4,1)S(1)} %iota_compare_fusion.5, bf16[4,64,32,128]{3,2,1,0:T(8,128)(2,1)S(1)} %get-tuple-element.178, s32[]{:T(128)S(6)} %copy.34), kind=kOutput, calls=%fused_computation.17.clone.1 | convolution fusion | flops 101447680 | bytes 3694596 | tf_op jit(solution)/shard_map/while/body/eval_jaxpr/uhv,uyv->uhy/dot_general | solution.py:34
  139.0 0.1 reduce_sum.113
  139.2 0.8 gather_fusion.1
  140.1 2.6 %gather_fusion = bf16[64,192,128]{2,1,0:T(8,128)(2,1)} fusion(bf16[16,192,128]{2,1,0:T(8,128)(2,1)S(1)} %get-tuple-element.179, s32[1024]{0:T(1024)S(1)} %pad_clamp_fusion.4), kind=kCustom, calls=%fused_computation.1.clone.1 | custom fusion | bytes 6291712 | tf_op jit(solution)/shard_map/while/body/eval_jaxpr/gather | solution.py:33
  142.7 4.1 %select_reduce_fusion.3 = f32[64,32]{1,0:T(8,128)S(1)} fusion(bf16[64,192,128]{2,1,0:T(8,128)(2,1)} %gather_fusion, pred[64,192]{1,0:T(8,128)(4,1)S(1)} %iota_compare_fusion.5, bf16[4,64,32,128]{3,2,1,0:T(8,128)(2,1)S(1)} %get-tuple-element.178, s32[]{:T(128)S(6)} %copy.34), kind=kOutput, calls=%fused_computation.17.clone.1 | convolution fusion | flops 101447680 | bytes 3694596 | tf_op jit(solution)/shard_map/while/body/eval_jaxpr/uhv,uyv->uhy/dot_general | solution.py:34
  146.7 0.1 reduce_sum.113
  146.9 0.7 all_to_all.18
  147.6 12.0 %all-to-all-start.2 = ((f32[64,1,4]{2,1,0:T(1,128)}), f32[64,1,4]{2,1,0:T(1,128)S(1)}, u32[]{:S(2)}, u32[]{:S(2)}) async-start(f32[64,1,4]{2,1,0:T(1,128)} %bitcast.22), calls=%async_computation.2 | async-start | bytes 65536 | tf_op jit(solution)/shard_map/all_to_all | solution.py:70
  159.6 0.5 fusion.19
  160.1 11.4 %all-to-all-done.2 = f32[64,1,4]{2,1,0:T(1,128)S(1)} async-done(((f32[64,1,4]{2,1,0:T(1,128)}), f32[64,1,4]{2,1,0:T(1,128)S(1)}, u32[]{:S(2)}, u32[]{:S(2)}) %all-to-all-start.2) | async-done | bytes 1056 | tf_op jit(solution)/shard_map/all_to_all | solution.py:70
  171.6 0.5 broadcast.345
  172.1 0.7 reduce.18
  172.8 0.1 reshape.292
  172.9 1.3 gather_fusion.3
  174.3 0.7 broadcast_in_dim_reshape.3
  174.9 0.1 exponential_reduce_fusion.1
  175.1 0.7 multiply_reduce_fusion
  (65 shorter events, 1.9 us)
Async XLA Ops:
  7.2 68.6 %all-gather.3.cloned.1.call-start = ((), (), s32[]{:S(2)}) async-start(), calls=%async_computation.3 | async-start | bytes 1769472 | tf_op jit(solution)/shard_map/all_gather | solution.py:117
  15.1 37.1 %all-to-all-start = ((s32[64,1,4]{2,1,0:T(1,128)}), s32[64,1,4]{2,1,0:T(1,128)S(1)}, u32[]{:S(2)}, u32[]{:S(2)}) async-start(s32[64,1,4]{2,1,0:T(1,128)} %bitcast.13), calls=%async_computation | async-start | bytes 65536 | tf_op jit(solution)/shard_map/all_to_all | solution.py:101
  52.2 12.8 %copy-start.2 = (f32[1,4,32]{2,1,0:T(4,128)S(1)}, f32[1,4,32]{2,1,0:T(4,128)}, u32[]{:S(2)}) copy-start(f32[1,4,32]{2,1,0:T(4,128)} %param.19) | copy-start | bytes 1540
  52.2 20.4 %copy-start.1 = (bf16[1,16,192,128]{3,2,1,0:T(8,128)(2,1)S(1)}, bf16[1,16,192,128]{3,2,1,0:T(8,128)(2,1)}, u32[]{:S(2)}) copy-start(bf16[1,16,192,128]{3,2,1,0:T(8,128)(2,1)} %param.13) | copy-start | bytes 2359300
  52.2 63.8 %all-to-all-start.1 = ((bf16[64,4,32,128]{3,2,1,0:T(8,128)(2,1)}), bf16[64,4,32,128]{3,2,1,0:T(8,128)(2,1)S(1)}, u32[]{:S(2)}, u32[]{:S(2)}) async-start(bf16[64,4,32,128]{3,2,1,0:T(8,128)(2,1)} %bitcast.18), calls=%async_computation.1 | async-start | bytes 4194304 | tf_op jit(solution)/shard_map/all_to_all | solution.py:100
  75.7 40.2 %copy-start = (s32[1,16]{1,0:T(1,128)S(1)}, s32[1,16]{1,0:T(1,128)}, u32[]{:S(2)}) copy-start(s32[1,16]{1,0:T(1,128)} %param.14) | copy-start | bytes 196
  147.6 24.0 %all-to-all-start.2 = ((f32[64,1,4]{2,1,0:T(1,128)}), f32[64,1,4]{2,1,0:T(1,128)S(1)}, u32[]{:S(2)}, u32[]{:S(2)}) async-start(f32[64,1,4]{2,1,0:T(1,128)} %bitcast.22), calls=%async_computation.2 | async-start | bytes 65536 | tf_op jit(solution)/shard_map/all_to_all | solution.py:70
Sparse Core Ops, SparseCore 0:
  10.3 32.8 all-gather.2
where the time goes:
time: 185 us; the launch traced here: 183 us
  waiting for transfers between devices  43.7 us (24%)
  starting transfers between devices  41.4 us (22%)
  local copies, waits for them, and re-layouts  39.6 us (21%)
  matrix products  22.2 us (12%)
  between operations  14.9 us (8%)
  other arithmetic  13.2 us (7%)
  blocking collectives  7.29 us (4%)
    all_to_all x1, waiting for transfers between devices, per_device(): lax.all_to_all(send_queries, 'dp', split_axis=0, concat_axis=0, tiled=True)  32.3 us
    all_to_all x1, starting transfers between devices, per_device(): lax.all_to_all(send_ids, 'dp', split_axis=0, concat_axis=0, tiled=True)  16.6 us
    dot_general x4, matrix products, slot_block_relevance(): jnp.einsum('uhv,uyv->uhy', query_tile_rows, document_rows, preferred_elem...  16.2 us
    scatter x1, local copies, waits for them, and re-layouts, per_device(): send_queries = jnp.zeros((peer_count * capacity,) + query_unit.shape[1:],...  13.7 us
    all_to_all x1, starting transfers between devices, per_device(): lax.all_to_all(send_queries, 'dp', split_axis=0, concat_axis=0, tiled=True)  12.8 us
    all_to_all x1, starting transfers between devices, send_back(): return lax.all_to_all(scored, 'dp', split_axis=0, concat_axis=0, tiled=True)  12 us
    all_to_all x1, waiting for transfers between devices, send_back(): return lax.all_to_all(scored, 'dp', split_axis=0, concat_axis=0, tiled=True)  11.4 us
    gather x4, local copies, waits for them, and re-layouts, slot_block_relevance(): document_rows = passage_unit[id_block]  10.5 us
  transfers between devices with their start and end apart: 4, of which 2 were waited for; matrix products, arithmetic and copies ran while one was open for 20% of the time, Pallas kernels for 0%

commit v1 on v0

v1 whole, which is shorter than its diff:
```python
import functools

import jax
import jax.numpy as jnp
from jax import lax
from jax.experimental import pallas as pl
from jax.experimental.pallas import tpu as pltpu
from jax.sharding import PartitionSpec as P

NEG = -1000000000.0


def unit_rows(values):
    wide = values.astype(jnp.float32)
    total = jnp.sum(wide * wide, axis=-1, keepdims=True) + 1e-06
    return (wide * lax.rsqrt(total)).astype(jnp.bfloat16)


def student_kernel(qrow_ref, pid_ref, len_ref, g_ref, p_ref, o_ref, *, slots):
    sources = g_ref.shape[0]
    qlen = o_ref.shape[1] // slots
    plen = p_ref.shape[1]
    lane_slot = lax.broadcasted_iota(jnp.int32, (1, o_ref.shape[1]), 1) // qlen
    row_ids = lax.broadcasted_iota(jnp.int32, (plen, o_ref.shape[1]), 0)

    def body(s, carry):
        pieces = []
        for r in range(slots):
            j = qrow_ref[s * slots + r]
            pieces.append(g_ref[s, pl.ds(pl.multiple_of(j * qlen, qlen), qlen), :])
        q = jnp.concatenate(pieces, axis=0)
        row = jnp.zeros((1, o_ref.shape[1]), jnp.float32)
        for r in range(slots):
            pidx = pid_ref[s * slots + r]
            sim = lax.dot_general(
                p_ref[pidx], q, (((1,), (1,)), ((), ())), preferred_element_type=jnp.float32
            )
            sim = jnp.where(row_ids < len_ref[pidx], sim, NEG)
            row = jnp.where(lane_slot == r, jnp.max(sim, axis=0, keepdims=True), row)
        o_ref[pl.ds(s, 1), :] = row
        return carry

    lax.fori_loop(0, sources, body, 0)


def student_scores(qrow, pid, lengths, gathered, passage_unit, slots, qlen):
    sources = gathered.shape[0]
    plen, dim = passage_unit.shape[1], passage_unit.shape[2]
    flops = 2 * sources * slots * plen * dim * slots * qlen
    return pl.pallas_call(
        functools.partial(student_kernel, slots=slots),
        out_shape=jax.ShapeDtypeStruct((sources, slots * qlen), jnp.float32),
        in_specs=[pl.BlockSpec(memory_space=pltpu.SMEM)] * 3
        + [pl.BlockSpec(memory_space=pltpu.VMEM)] * 2,
        out_specs=pl.BlockSpec(memory_space=pltpu.VMEM),
        cost_estimate=pl.CostEstimate(
            flops=flops,
            transcendentals=0,
            bytes_accessed=gathered.size * 2 + passage_unit.size * 2 + sources * slots * qlen * 4,
        ),
    )(qrow, pid, lengths, gathered, passage_unit)


def cross_kernel(len_ref, q_ref, p_ref, o_ref):
    plen = p_ref.shape[1]
    row_ids = lax.broadcasted_iota(jnp.int32, (plen, q_ref.shape[0]), 0)
    q = q_ref[...]
    for k in range(p_ref.shape[0]):
        sim = lax.dot_general(
            p_ref[k], q, (((1,), (1,)), ((), ())), preferred_element_type=jnp.float32
        )
        sim = jnp.where(row_ids < len_ref[k], sim, NEG)
        o_ref[pl.ds(k, 1), :] = jnp.max(sim, axis=0, keepdims=True)


def cross_scores(lengths, query_rows, positive_unit):
    docs, plen, dim = positive_unit.shape
    cols = query_rows.shape[0]
    return pl.pallas_call(
        cross_kernel,
        out_shape=jax.ShapeDtypeStruct((docs, cols), jnp.float32),
        in_specs=[pl.BlockSpec(memory_space=pltpu.SMEM)]
        + [pl.BlockSpec(memory_space=pltpu.VMEM)] * 2,
        out_specs=pl.BlockSpec(memory_space=pltpu.VMEM),
        cost_estimate=pl.CostEstimate(
            flops=2 * docs * plen * dim * cols,
            transcendentals=0,
            bytes_accessed=query_rows.size * 2 + positive_unit.size * 2 + docs * cols * 4,
        ),
    )(lengths, query_rows, positive_unit)


def per_device(
    queries, passages, passage_lengths, positives, positive_lengths, owners, local_ids, teacher
):
    peer_count = lax.axis_size("dp")
    me = lax.axis_index("dp")
    query_count, qlen, dim = queries.shape[1], queries.shape[2], queries.shape[3]
    cand_count = owners.shape[2]
    pass_count = passages.shape[1]
    pairs = query_count * cand_count
    slots = 4

    query_unit = unit_rows(queries[0]).reshape(query_count * qlen, dim)
    id_rows = jnp.stack(
        [
            jnp.clip(owners[0, :, :, 0].reshape(pairs), 0, peer_count - 1),
            jnp.clip(local_ids[0].reshape(pairs), 0, pass_count - 1),
        ]
    ).astype(jnp.bfloat16)
    id_rows = id_rows.reshape(2 * pairs // dim, dim)
    id_block = jnp.zeros((16, dim), jnp.bfloat16).at[: id_rows.shape[0]].set(id_rows)
    send = jnp.concatenate([query_unit, id_block], axis=0)

    column_queries = lax.all_gather(query_unit, "blk", axis=0, tiled=True)
    positive_unit = unit_rows(positives[0])
    column_scores = cross_scores(positive_lengths[0], column_queries, positive_unit)
    groups = lax.axis_size("blk")
    column_scores = jnp.sum(
        column_scores.reshape(query_count, groups, query_count, qlen), axis=-1
    )
    every_scores = lax.all_gather(column_scores, "blk", axis=0)
    mine = lax.dynamic_index_in_dim(every_scores, lax.axis_index("blk"), axis=2, keepdims=False)
    logits = jnp.transpose(mine, (2, 0, 1)).reshape(query_count, groups * query_count)
    own_column = lax.axis_index("blk") * query_count + jnp.arange(query_count, dtype=jnp.int32)
    own_logit = jnp.take_along_axis(logits, own_column[:, None], axis=1)[:, 0]
    contrast = jnp.log(jnp.sum(jnp.exp(logits), axis=-1)) - own_logit

    gathered = lax.all_gather(send, "dp", axis=0)
    ids = gathered[:, query_count * qlen : query_count * qlen + 2 * pairs // dim, :]
    ids = ids.reshape(peer_count, 2, pairs).astype(jnp.int32)
    pair_owner, pair_local = ids[:, 0, :], ids[:, 1, :]
    hit = (pair_owner == me).astype(jnp.int32)
    rank = jnp.cumsum(hit, axis=1) - hit
    pair_index = lax.broadcasted_iota(jnp.int32, (peer_count, pairs), 1)
    chosen = [(hit > 0) & (rank == r) for r in range(slots)]
    slot_pair = jnp.stack([jnp.sum(jnp.where(c, pair_index, 0), axis=1) for c in chosen], axis=1)
    slot_local = jnp.stack([jnp.sum(jnp.where(c, pair_local, 0), axis=1) for c in chosen], axis=1)
    qrow = (slot_pair // cand_count).reshape(-1)
    passage_unit = unit_rows(passages[0])
    raw = student_scores(
        qrow,
        slot_local.reshape(-1),
        passage_lengths[0],
        gathered,
        passage_unit,
        slots,
        qlen,
    )
    slot_score = jnp.sum(raw.reshape(peer_count, slots, qlen), axis=-1)
    placed = jnp.zeros((peer_count, pairs), jnp.float32)
    for r in range(slots):
        placed = placed + jnp.where(chosen[r], slot_score[:, r : r + 1], 0.0)
    returned = lax.psum_scatter(placed, "dp", scatter_dimension=0, tiled=True)
    student = returned.reshape(query_count, cand_count)

    teacher_score_rows = teacher[0]
    log_teacher = teacher_score_rows - jnp.log(
        jnp.sum(jnp.exp(teacher_score_rows), axis=-1, keepdims=True)
    )
    log_student = student - jnp.log(jnp.sum(jnp.exp(student), axis=-1, keepdims=True))
    distill = jnp.sum(jnp.exp(log_teacher) * (log_teacher - log_student), axis=-1)
    return (student[None], distill[None], contrast[None])


def solution(mesh):
    in_specs = (
        P("blk", "dp", None, None),
        P("blk", "dp", None, None),
        P("blk", "dp"),
        P("blk", "dp", None, None),
        P("blk", "dp"),
        P("blk", "dp", None, None),
        P("blk", "dp", None),
        P("blk", "dp", None),
    )
    out_specs = (P("blk", "dp", None), P("blk", "dp"), P("blk", "dp"))
    return jax.shard_map(
        per_device, mesh=mesh, in_specs=in_specs, out_specs=out_specs, check_vma=False
    )
```

time: 185 us -> 408 us (2.21)
  blocking collectives: 7.29 us -> 306 us
  starting transfers between devices: 41.4 us -> 0.04 us
  local copies, waits for them, and re-layouts: 39.6 us -> 6.9 us
  matrix products: 22.2 us -> 0 us
  Pallas kernels: 0 us -> 19.7 us
    unnamed x1, blocking collectives: 7.29 us -> 277 us
    all_gather x1, waiting for transfers between devices: 0.02 us -> 47.3 us  [per_device(): gathered = lax.all_gather(send, 'dp', axis=0)]
    all_to_all x3 -> x0, waiting for transfers between devices: 43.7 us -> none  [the longest x1 32.3 us: per_device(): lax.all_to_all(send_queries, 'dp', split_axis=0, concat_axis=0, tiled=True)]
    all_to_all x3 -> x0, starting transfers between devices: 41.4 us -> none  [the longest x1 16.6 us: per_device(): lax.all_to_all(send_ids, 'dp', split_axis=0, concat_axis=0, tiled=True)]
    all_gather x0 -> x2, blocking collectives: none -> 29.6 us  [the longest x1 16.6 us: per_device(): column_queries = lax.all_gather(query_unit, 'blk', axis=0, tiled=True)]
    dot_general x8 -> x0, matrix products: 22.2 us -> none  [the longest x4 16.2 us: slot_block_relevance(): jnp.einsum('uhv,uyv->uhy', query_tile_rows, document_rows, preferred_elem...]
    pallas_call x0 -> x2, Pallas kernels: none -> 19.7 us  [the longest x1 17.5 us: student_scores(): pl.pallas_call(functools.partial(student_kernel, slots=slots), out_shape=...]
    gather x11 -> x1, local copies, waits for them, and re-layouts: 16.2 us -> 0.65 us  [per_device(): own_logit = jnp.take_along_axis(logits, own_column[:, None], axis=1)[:, 0]]
  transfers between devices with their start and end apart: 4 -> 1, of which waited for: 2 -> 1; matrix products, arithmetic and copies ran while one was open for 20% -> 2% of each run, Pallas kernels for 0% -> 1%
where the time goes in v1:
time: 408 us
  blocking collectives  306 us (75%)
  waiting for transfers between devices  47.3 us (12%)
  Pallas kernels  19.7 us (5%)
  between operations  14.2 us (3%)
  other arithmetic  13.3 us (3%)
  local copies, waits for them, and re-layouts  6.9 us (2%)
    unnamed x1, blocking collectives  277 us
    all_gather x1, waiting for transfers between devices, per_device(): gathered = lax.all_gather(send, 'dp', axis=0)  47.3 us
    pallas_call x1, Pallas kernels, student_scores(): pl.pallas_call(functools.partial(student_kernel, slots=slots), out_shape=...  17.5 us
    all_gather x1, blocking collectives, per_device(): column_queries = lax.all_gather(query_unit, 'blk', axis=0, tiled=True)  16.6 us
    all_gather x1, blocking collectives, per_device(): every_scores = lax.all_gather(column_scores, 'blk', axis=0)  13 us
  transfers between devices with their start and end apart: 1, of which 1 were waited for; matrix products, arithmetic and copies ran while one was open for 2% of the time, Pallas kernels for 1%

profile of v1, /device:TPU:6, one launch (start us, length us, event | category | flops | bytes accessed | tf_op | source)
XLA Modules:
  0.0 407.8 jit_solution(16489479598053681398)
XLA Ops:
  7.2 0.0 copy-start
  7.2 0.0 all-gather.4.cloned.1.call-start
  7.2 0.8 convert_reduce_fusion
  8.0 0.1 min.20
  8.1 0.7 clamp_convert_fusion
  8.8 0.1 min.23
  8.9 0.8 multiply_reduce_fusion
  9.7 0.1 rsqrt.28
  9.8 0.8 fusion.4
  10.7 0.6 pad_maximum_fusion
  11.3 0.0 all-gather.4.cloned.1.call-update
  11.3 0.8 fusion.8
  12.1 16.6 %all_gather.17.q_ref = bf16[1024,128]{1,0:T(8,128)(2,1)} all-gather(bf16[128,128]{1,0:T(8,128)(2,1)S(1)} %fusion.4), channel_id=1, replica_groups=mesh['dp'=64,'blk'=8] {'blk'}, dimensions={0}, use_global_device_ids=true | all-gather | bytes 294912 | tf_op jit(solution)/shard_map/all_gather | solution.py:115
  28.7 1.1 fusion.2
  29.9 1.8 fusion.3.p_ref
  31.6 2.2 shard_map.104
  33.8 0.8 reshape.206
  34.7 0.1 reduce_sum.168
  34.8 0.1 copy.23
  34.9 13.0 %all-gather.1 = f32[32,8,4]{1,2,0:T(4,128)S(1)} all-gather(f32[4,8,4]{1,2,0:T(4,128)S(1)} %copy.23), channel_id=3, replica_groups=mesh['dp'=64,'blk'=8] {'blk'}, dimensions={0}, use_global_device_ids=true | all-gather | bytes 4608 | tf_op jit(solution)/shard_map/all_gather | solution.py:122
  47.9 0.1 constant_dynamic-slice_fusion.1
  48.0 0.2 copy.25
  48.2 0.1 copy.26
  48.3 0.1 reshape.207
  48.4 1.3 dynamic-slice.7
  49.7 0.6 gather_fusion
  50.3 0.1 exponential_reduce_fusion
  50.5 0.0 copy-done
  50.5 0.6 fusion
  51.1 0.5 fusion.9
  51.6 1.4 fusion.1.p_ref
  53.0 47.3 %all-gather.4.cloned.1.call-done = bf16[9216,128]{1,0:T(8,128)(2,1)} async-done(((bf16[144,128]{1,0:T(8,128)(2,1)}), bf16[9216,128]{1,0:T(8,128)(2,1)}) %all-gather.4.cloned.1.call-update) | async-done | bytes 2359312 | tf_op jit(solution)/shard_map/all_gather | solution.py:129
  100.3 0.9 slice_convert_fusion
  101.3 0.1 fusion.12
  101.3 0.3 reduce_window_sum.11
  101.6 0.2 select_reduce_fusion.3
  101.9 0.1 copy.20
  102.0 0.1 stack.44
  102.1 0.6 and_select_fusion.1.qrow_ref
  102.7 0.1 copy.21
  102.8 0.7 reshape.203.pid_ref
  103.5 0.0 copy-start.1
  103.5 17.5 %shard_map.103 = f32[64,128]{1,0:T(8,128)} custom-call(s32[256]{0:T(256)} %and_select_fusion.1.qrow_ref, s32[256]{0:T(256)} %reshape.203.pid_ref, s32[16]{0:T(128)} %bitcast.78, bf16[64,144,128]{2,1,0:T(8,128)(2,1)} %bitcast.76, bf16[16,192,128]{2,1,0:T(8,128)(2,1)} %fusion.1.p_ref), custom_call_target="tpu_custom_call" | custom-call | flops 1610612736 | bytes 3178496 | tf_op jit(solution)/shard_map/pallas_call | solution.py:50
  121.0 0.8 copy.22
  121.9 0.1 select_add_fusion
  122.0 276.7 %all-reduce.1 = f32[64,128]{1,0:T(8,128)S(1)} all-reduce(f32[64,128]{1,0:T(8,128)S(1)} %select_add_fusion), channel_id=4, replica_groups=mesh['dp'=64,'blk'=8] {'dp'}, use_global_device_ids=true, to_apply=%region_12.13.clone | all-reduce | flops 8192 | bytes 65536
  398.7 0.7 fusion.11
  399.3 0.1 reshape.205
  399.4 0.1 exponential_reduce_fusion.1
  399.5 0.7 broadcast_in_dim_reshape.3
  400.2 0.0 copy-done.1
  400.2 0.7 multiply_reduce_fusion.1
  (16 shorter events, 0.1 us)
Async XLA Ops:
  7.2 43.3 %copy-start = (bf16[1,16,192,128]{3,2,1,0:T(8,128)(2,1)S(1)}, bf16[1,16,192,128]{3,2,1,0:T(8,128)(2,1)}, u32[]{:S(2)}) copy-start(bf16[1,16,192,128]{3,2,1,0:T(8,128)(2,1)} %param.11) | copy-start | bytes 2359300
  7.2 93.1 %all-gather.4.cloned.1.call-start = ((), (), s32[]{:S(2)}) async-start(), calls=%async_computation | async-start | bytes 2396160 | tf_op jit(solution)/shard_map/all_gather | solution.py:129
  103.5 296.7 %copy-start.1 = (f32[1,4,32]{2,1,0:T(4,128)S(1)}, f32[1,4,32]{2,1,0:T(4,128)}, u32[]{:S(2)}) copy-start(f32[1,4,32]{2,1,0:T(4,128)} %param.17) | copy-start | bytes 1540
Sparse Core Ops, SparseCore 0:
  11.4 88.8 all-gather.3

commit v2 on v1

v2 whole, which is shorter than its diff:
```python
import functools

import jax
import jax.numpy as jnp
from jax import lax
from jax.experimental import pallas as pl
from jax.experimental.pallas import tpu as pltpu
from jax.sharding import PartitionSpec as P

NEG = -1000000000.0


def unit_rows(values):
    wide = values.astype(jnp.float32)
    total = jnp.sum(wide * wide, axis=-1, keepdims=True) + 1e-06
    return (wide * lax.rsqrt(total)).astype(jnp.bfloat16)


def student_kernel(n_ref, gpid_ref, gsrc_ref, grow_ref, len_ref, g_ref, p_ref, o_ref):
    lanes = o_ref.shape[1]
    slots = gsrc_ref.shape[0] // o_ref.shape[0]
    qlen = lanes // slots
    plen = p_ref.shape[1]
    row_ids = lax.broadcasted_iota(jnp.int32, (plen, lanes), 0)

    def body(g, carry):
        pieces = []
        for r in range(slots):
            src = gsrc_ref[g * slots + r]
            j = grow_ref[g * slots + r]
            pieces.append(g_ref[src, pl.ds(pl.multiple_of(j * qlen, qlen), qlen), :])
        q = jnp.concatenate(pieces, axis=0)
        pidx = gpid_ref[g]
        sim = lax.dot_general(
            p_ref[pidx], q, (((1,), (1,)), ((), ())), preferred_element_type=jnp.float32
        )
        sim = jnp.where(row_ids < len_ref[pidx], sim, NEG)
        o_ref[pl.ds(g, 1), :] = jnp.max(sim, axis=0, keepdims=True)
        return carry

    lax.fori_loop(0, n_ref[0], body, 0)


def student_scores(n_groups, gpid, gsrc, grow, lengths, gathered, passage_unit, group_cap, lanes):
    plen, dim = passage_unit.shape[1], passage_unit.shape[2]
    return pl.pallas_call(
        student_kernel,
        out_shape=jax.ShapeDtypeStruct((group_cap, lanes), jnp.float32),
        in_specs=[pl.BlockSpec(memory_space=pltpu.SMEM)] * 5
        + [pl.BlockSpec(memory_space=pltpu.VMEM)] * 2,
        out_specs=pl.BlockSpec(memory_space=pltpu.VMEM),
        cost_estimate=pl.CostEstimate(
            flops=2 * group_cap * plen * dim * lanes,
            transcendentals=0,
            bytes_accessed=gathered.size * 2 + passage_unit.size * 2 + group_cap * lanes * 4,
        ),
    )(n_groups, gpid, gsrc, grow, lengths, gathered, passage_unit)


def cross_kernel(len_ref, q_ref, p_ref, o_ref, *, plen):
    groups = p_ref.shape[0]
    docs = o_ref.shape[0] // groups
    row_ids = lax.broadcasted_iota(jnp.int32, (plen, q_ref.shape[0]), 0)
    q = q_ref[...]
    for e in range(groups):
        for k in range(docs):
            sim = lax.dot_general(
                p_ref[e, k * plen : (k + 1) * plen, :],
                q,
                (((1,), (1,)), ((), ())),
                preferred_element_type=jnp.float32,
            )
            sim = jnp.where(row_ids < len_ref[e * docs + k], sim, NEG)
            o_ref[pl.ds(e * docs + k, 1), :] = jnp.max(sim, axis=0, keepdims=True)


def cross_scores(lengths, query_rows, gathered_docs, doc_count, plen):
    groups, rows, dim = gathered_docs.shape
    cols = query_rows.shape[0]
    return pl.pallas_call(
        functools.partial(cross_kernel, plen=plen),
        out_shape=jax.ShapeDtypeStruct((groups * doc_count, cols), jnp.float32),
        in_specs=[pl.BlockSpec(memory_space=pltpu.SMEM)]
        + [pl.BlockSpec(memory_space=pltpu.VMEM)] * 2,
        out_specs=pl.BlockSpec(memory_space=pltpu.VMEM),
        cost_estimate=pl.CostEstimate(
            flops=2 * groups * rows * dim * cols,
            transcendentals=0,
            bytes_accessed=query_rows.size * 2 + gathered_docs.size * 2 + groups * doc_count * cols * 4,
        ),
    )(lengths, query_rows, gathered_docs)


def per_device(
    queries, passages, passage_lengths, positives, positive_lengths, owners, local_ids, teacher
):
    peer_count = lax.axis_size("dp")
    me = lax.axis_index("dp")
    query_count, qlen, dim = queries.shape[1], queries.shape[2], queries.shape[3]
    cand_count = owners.shape[2]
    pass_count, plen = passages.shape[1], passages.shape[2]
    pairs = query_count * cand_count
    slots = 4
    lanes = slots * qlen
    group_cap = peer_count * slots // slots + pass_count

    positive_unit = unit_rows(positives[0]).reshape(query_count * plen, dim)
    length_row = jnp.zeros((16, dim), jnp.bfloat16).at[0, :query_count].set(
        positive_lengths[0].astype(jnp.bfloat16)
    )
    doc_block = jnp.concatenate([positive_unit, length_row], axis=0)
    column_docs = lax.all_gather(doc_block, "blk", axis=0)
    groups = column_docs.shape[0]
    doc_lengths = column_docs[:, query_count * plen, :query_count].astype(jnp.int32).reshape(-1)

    query_unit = unit_rows(queries[0]).reshape(query_count * qlen, dim)
    id_rows = jnp.stack(
        [
            jnp.clip(owners[0, :, :, 0].reshape(pairs), 0, peer_count - 1),
            jnp.clip(local_ids[0].reshape(pairs), 0, pass_count - 1),
        ]
    ).astype(jnp.bfloat16)
    id_rows = id_rows.reshape(2 * pairs // dim, dim)
    id_block = jnp.zeros((16, dim), jnp.bfloat16).at[: id_rows.shape[0]].set(id_rows)
    send = jnp.concatenate([query_unit, id_block], axis=0)
    gathered = lax.all_to_all(
        jnp.broadcast_to(send[None], (peer_count,) + send.shape),
        "dp",
        split_axis=0,
        concat_axis=0,
        tiled=True,
    )

    raw_cross = cross_scores(doc_lengths, query_unit, column_docs, query_count, plen)
    logits = jnp.sum(raw_cross.reshape(groups * query_count, query_count, qlen), axis=-1).T
    own_column = lax.axis_index("blk") * query_count + jnp.arange(query_count, dtype=jnp.int32)
    own_logit = jnp.take_along_axis(logits, own_column[:, None], axis=1)[:, 0]
    contrast = jnp.log(jnp.sum(jnp.exp(logits), axis=-1)) - own_logit

    ids = gathered[:, query_count * qlen : query_count * qlen + 2 * pairs // dim, :]
    ids = ids.reshape(peer_count, 2, pairs).astype(jnp.int32)
    pair_owner, pair_local = ids[:, 0, :], ids[:, 1, :]
    hit = (pair_owner == me).astype(jnp.int32)
    rank = jnp.cumsum(hit, axis=1) - hit
    pair_index = lax.broadcasted_iota(jnp.int32, (peer_count, pairs), 1)
    chosen = [(hit > 0) & (rank == r) for r in range(slots)]
    slot_pair = jnp.stack([jnp.sum(jnp.where(c, pair_index, 0), axis=1) for c in chosen], axis=1)
    slot_local = jnp.stack([jnp.sum(jnp.where(c, pair_local, 0), axis=1) for c in chosen], axis=1)
    slot_valid = jnp.stack([jnp.any(c, axis=1) for c in chosen], axis=1).reshape(-1)
    slot_pid = slot_local.reshape(-1)
    slot_src = (lax.broadcasted_iota(jnp.int32, (peer_count, slots), 0)).reshape(-1)
    slot_row = (slot_pair // cand_count).reshape(-1)

    by_pass = (
        slot_valid[:, None] & (slot_pid[:, None] == jnp.arange(pass_count, dtype=jnp.int32)[None, :])
    ).astype(jnp.int32)
    per_pass = jnp.sum(by_pass, axis=0)
    pass_groups = (per_pass + slots - 1) // slots
    pass_base = jnp.cumsum(pass_groups) - pass_groups
    n_groups = jnp.sum(pass_groups).reshape(1)
    in_pass = jnp.sum((jnp.cumsum(by_pass, axis=0) - by_pass) * by_pass, axis=1)
    slot_target = jnp.sum(pass_base[None, :] * by_pass, axis=1) * slots + in_pass
    slot_target = jnp.where(slot_valid, slot_target, group_cap * slots)
    target_hit = slot_target[None, :] == jnp.arange(group_cap * slots, dtype=jnp.int32)[:, None]
    gsrc = jnp.sum(jnp.where(target_hit, slot_src[None, :], 0), axis=1)
    grow = jnp.sum(jnp.where(target_hit, slot_row[None, :], 0), axis=1)
    group_index = jnp.arange(group_cap, dtype=jnp.int32)[:, None]
    gpid = jnp.sum(
        jnp.where(
            (group_index >= pass_base[None, :]) & (group_index < (pass_base + pass_groups)[None, :]),
            jnp.arange(pass_count, dtype=jnp.int32)[None, :],
            0,
        ),
        axis=1,
    )
    passage_unit = unit_rows(passages[0])
    raw = student_scores(
        n_groups, gpid, gsrc, grow, passage_lengths[0], gathered, passage_unit, group_cap, lanes
    )
    group_score = jnp.sum(raw.reshape(group_cap * slots, qlen), axis=-1)
    slot_score = jnp.take(group_score, jnp.minimum(slot_target, group_cap * slots - 1))
    slot_score = jnp.where(slot_valid, slot_score, 0.0).reshape(peer_count, slots)
    returned = lax.all_to_all(slot_score, "dp", split_axis=0, concat_axis=0, tiled=True)

    my_owner = jnp.clip(owners[0, :, :, 0].reshape(pairs), 0, peer_count - 1)
    owner_hot = (my_owner[:, None] == jnp.arange(peer_count, dtype=jnp.int32)[None, :]).astype(
        jnp.int32
    )
    my_rank = jnp.sum((jnp.cumsum(owner_hot, axis=0) - owner_hot) * owner_hot, axis=1)
    student = returned[my_owner, jnp.minimum(my_rank, slots - 1)].reshape(query_count, cand_count)

    teacher_score_rows = teacher[0]
    log_teacher = teacher_score_rows - jnp.log(
        jnp.sum(jnp.exp(teacher_score_rows), axis=-1, keepdims=True)
    )
    log_student = student - jnp.log(jnp.sum(jnp.exp(student), axis=-1, keepdims=True))
    distill = jnp.sum(jnp.exp(log_teacher) * (log_teacher - log_student), axis=-1)
    return (student[None], distill[None], contrast[None])


def solution(mesh):
    in_specs = (
        P("blk", "dp", None, None),
        P("blk", "dp", None, None),
        P("blk", "dp"),
        P("blk", "dp", None, None),
        P("blk", "dp"),
        P("blk", "dp", None, None),
        P("blk", "dp", None),
        P("blk", "dp", None),
    )
    out_specs = (P("blk", "dp", None), P("blk", "dp"), P("blk", "dp"))
    return jax.shard_map(
        per_device, mesh=mesh, in_specs=in_specs, out_specs=out_specs, check_vma=False
    )
```

time: 408 us -> 142 us (0.35)
  blocking collectives: 306 us -> 0 us
  starting transfers between devices: 0.04 us -> 23.1 us
  waiting for transfers between devices: 47.3 us -> 61.9 us
  local copies, waits for them, and re-layouts: 6.9 us -> 11.9 us
    unnamed x1 -> x0, blocking collectives: 277 us -> none
    all_to_all x0 -> x2, waiting for transfers between devices: none -> 34.1 us  [the longest x1 22.6 us: per_device(): lax.all_to_all(jnp.broadcast_to(send[None], (peer_count,) + send.shape),...]
    all_gather x2 -> x0, blocking collectives: 29.6 us -> none  [the longest x1 16.6 us: per_device(): column_queries = lax.all_gather(query_unit, 'blk', axis=0, tiled=True)]
    all_to_all x0 -> x2, starting transfers between devices: none -> 23 us  [the longest x1 16.7 us: per_device(): lax.all_to_all(jnp.broadcast_to(send[None], (peer_count,) + send.shape),...]
    all_gather x1, waiting for transfers between devices: 47.3 us -> 27.8 us  [per_device(): column_docs = lax.all_gather(doc_block, 'blk', axis=0)]
  transfers between devices with their start and end apart: 1 -> 3, of which waited for: 1 -> 3; matrix products, arithmetic and copies ran while one was open for 2% -> 5% of each run, Pallas kernels for 1% -> 2%
where the time goes in v2:
time: 142 us
  waiting for transfers between devices  61.9 us (44%)
  starting transfers between devices  23.1 us (16%)
  Pallas kernels  17.4 us (12%)
  between operations  14.4 us (10%)
  other arithmetic  13.1 us (9%)
  local copies, waits for them, and re-layouts  11.9 us (8%)
    all_gather x1, waiting for transfers between devices, per_device(): column_docs = lax.all_gather(doc_block, 'blk', axis=0)  27.8 us
    all_to_all x1, waiting for transfers between devices, per_device(): lax.all_to_all(jnp.broadcast_to(send[None], (peer_count,) + send.shape),...  22.6 us
    all_to_all x1, starting transfers between devices, per_device(): lax.all_to_all(jnp.broadcast_to(send[None], (peer_count,) + send.shape),...  16.7 us
    pallas_call x1, Pallas kernels, student_scores(): pl.pallas_call(student_kernel, out_shape=jax.ShapeDtypeStruct((group_cap,...  14.6 us
    all_to_all x1, waiting for transfers between devices, per_device(): lax.all_to_all(slot_score, 'dp', split_axis=0, concat_axis=0, tiled=True)  11.4 us
    all_to_all x1, starting transfers between devices, per_device(): lax.all_to_all(slot_score, 'dp', split_axis=0, concat_axis=0, tiled=True)  6.31 us
    pallas_call x1, Pallas kernels, cross_scores(): pl.pallas_call(functools.partial(cross_kernel, plen=plen), out_shape=jax....  2.86 us
  transfers between devices with their start and end apart: 3, of which 3 were waited for; matrix products, arithmetic and copies ran while one was open for 5% of the time, Pallas kernels for 2%

profile of v2, /device:TPU:6, one launch (start us, length us, event | category | flops | bytes accessed | tf_op | source)
XLA Modules:
  0.0 141.8 jit_solution(8868334577335432631)
XLA Ops:
  7.2 0.8 multiply_reduce_fusion.1
  8.0 0.1 rsqrt.31
  8.1 0.8 fusion.5.q_ref
  9.0 0.7 convert_reduce_fusion.1
  9.7 0.1 min.69
  9.8 0.7 clamp_convert_fusion
  10.5 0.1 min.72
  10.6 1.7 %broadcast_in_dim.87 = bf16[64,144,128]{2,1,0:T(8,128)(2,1)} broadcast(bf16[144,128]{1,0:T(8,128)(2,1)S(1)} %pad_maximum_fusion), dimensions={1,2} | broadcast | bytes 2396160 | tf_op jit(solution)/shard_map/broadcast_in_dim | solution.py:127
  12.3 16.7 %all-to-all-start = ((bf16[64,144,128]{2,1,0:T(8,128)(2,1)}), bf16[64,144,128]{2,1,0:T(8,128)(2,1)S(1)}, u32[]{:S(2)}, u32[]{:S(2)}) async-start(bf16[64,144,128]{2,1,0:T(8,128)(2,1)} %broadcast_in_dim.87), calls=%async_computation | async-start | bytes 4718592 | tf_op jit(solution)/shard_map/all_to_all | solution.py:126
  29.1 0.2 multiply_reduce_fusion
  29.5 0.2 fusion.3
  29.6 0.7 fusion.4
  30.4 0.1 broadcast_in_dim.92
  30.5 0.1 min.78
  30.7 0.1 fusion.17
  30.8 0.1 fusion.6
  30.9 0.2 reduce_window_sum.47
  31.1 0.2 select_reduce_fusion.2
  31.3 0.6 fusion
  32.0 1.4 fusion.1.p_ref
  33.3 27.8 %all-gather.3.cloned.1.call-done = bf16[6272,128]{1,0:T(8,128)(2,1)} async-done(((bf16[784,128]{1,0:T(8,128)(2,1)}), bf16[6272,128]{1,0:T(8,128)(2,1)}) %all-gather.3.cloned.1.call-update) | async-done | bytes 1605648 | tf_op jit(solution)/shard_map/all_gather | solution.py:112
  61.1 0.7 fusion.16
  61.9 0.6 reshape.671.len_ref
  62.5 2.9 %shard_map.104 = f32[32,128]{1,0:T(8,128)} custom-call(s32[32]{0:T(128)} %reshape.671.len_ref, bf16[128,128]{1,0:T(8,128)(2,1)} %copy-done.3, bf16[8,784,128]{2,1,0:T(8,128)(2,1)} %bitcast.87), custom_call_target="tpu_custom_call" | custom-call | flops 205520896 | bytes 1654784 | tf_op jit(solution)/shard_map/pallas_call | solution.py:80
  65.3 0.8 reshape.666
  66.1 0.1 reduce_sum.248
  66.2 0.6 gather_fusion.2
  66.9 22.6 %all-to-all-done.g_ref = bf16[64,144,128]{2,1,0:T(8,128)(2,1)S(1)} async-done(((bf16[64,144,128]{2,1,0:T(8,128)(2,1)}), bf16[64,144,128]{2,1,0:T(8,128)(2,1)S(1)}, u32[]{:S(2)}, u32[]{:S(2)}) %all-to-all-start) | async-done | bytes 2359328 | tf_op jit(solution)/shard_map/all_to_all | solution.py:126
  89.6 0.3 reduce_window_sum.44
  89.9 0.1 fusion.27
  90.1 0.2 fusion.28
  90.2 0.2 select_reduce_fusion.10
  90.5 0.1 copy.39
  90.6 0.1 eq.92
  90.7 0.1 eq.88
  90.8 0.1 copy.38
  90.9 0.1 and.123
  91.0 0.1 and.118
  91.1 0.1 reshape.664
  91.3 0.1 copy.45
  91.4 0.1 stack.84
  91.5 0.6 reduce-window.18
  92.1 0.2 slice_reduce_fusion
  92.3 0.1 convert_reduce_fusion
  92.4 0.1 copy.40
  92.6 0.1 reduce.7
  92.7 0.6 select_reduce_fusion.12.gpid_ref
  93.3 0.1 select_reduce_fusion.11
  93.4 0.1 add.236
  93.6 0.6 reduce_sum.233
  94.2 0.8 select_reduce_fusion
  95.0 14.6 %shard_map.103 = f32[80,128]{1,0:T(8,128)} custom-call(s32[1]{0:T(128)} %bitcast.17.n_ref, s32[80]{0:T(128)} %select_reduce_fusion.12.gpid_ref, s32[320]{0:T(512)} %get-tuple-element.38.gsrc_ref, s32[320]{0:T(512)} %get-tuple-element.37.grow_ref, s32[16]{0:T(128)} %bitcast.110, bf16[64,144,128]{2,1,0:T(8,128)(2,1)} %copy-done, bf16[16,192,128]{2,1,0:T(8,128)(2,1)} %fusion.1.p_ref), custom_call_target="tpu_custom_call" | custom-call | flops 503316480 | bytes 3186688 | tf_op jit(solution)/shard_map/pallas_call | solution.py:46
  109.5 0.9 reshape.663
  110.4 0.1 reduce_sum.242
  110.6 2.0 %gather_fusion = f32[256]{0:T(256)S(1)} fusion(f32[320]{0:T(512)S(1)} %reduce_sum.242, s32[1024]{0:T(1024)S(1)} %pad_clamp_fusion), kind=kCustom, calls=%fused_computation | custom fusion | bytes 3072 | tf_op jit(solution)/shard_map/jit(_take)/gather | solution.py:181
  112.5 0.1 gather.16
  112.8 0.7 copy.48
  113.5 6.3 %all-to-all-start.1 = ((f32[64,1,4]{2,1,0:T(1,128)}), f32[64,1,4]{2,1,0:T(1,128)S(1)}, u32[]{:S(2)}, u32[]{:S(2)}) async-start(f32[64,1,4]{2,1,0:T(1,128)} %copy.48), calls=%async_computation.1 | async-start | bytes 65536 | tf_op jit(solution)/shard_map/all_to_all | solution.py:183
  119.8 0.5 fusion.18
  120.4 11.4 %all-to-all-done.1 = f32[64,1,4]{2,1,0:T(1,128)S(1)} async-done(((f32[64,1,4]{2,1,0:T(1,128)}), f32[64,1,4]{2,1,0:T(1,128)S(1)}, u32[]{:S(2)}, u32[]{:S(2)}) %all-to-all-start.1) | async-done | bytes 1056 | tf_op jit(solution)/shard_map/all_to_all | solution.py:183
  131.9 1.5 %gather_fusion.1 = f32[128]{0:T(128)S(1)} fusion(f32[64,4]{0,1:T(4,128)S(1)} %bitcast.84, s32[128]{0:T(128)S(1)} %fusion.24), kind=kCustom, calls=%fused_computation.1 | custom fusion | bytes 2048 | tf_op jit(solution)/shard_map/gather | solution.py:190
  133.5 0.7 broadcast_in_dim_reshape.2
  134.1 0.1 exponential_reduce_fusion.1
  134.3 0.7 multiply_reduce_fusion.2
  (54 shorter events, 1.0 us)
Async XLA Ops:
  9.0 3.4 %copy-start.3 = (bf16[128,128]{1,0:T(8,128)(2,1)}, bf16[128,128]{1,0:T(8,128)(2,1)S(1)}, u32[]{:S(2)}) copy-start(bf16[128,128]{1,0:T(8,128)(2,1)S(1)} %fusion.5.q_ref) | copy-start | bytes 98308
  12.3 16.8 %copy-start.2 = (bf16[1,4,192,128]{3,2,1,0:T(8,128)(2,1)S(1)}, bf16[1,4,192,128]{3,2,1,0:T(8,128)(2,1)}, u32[]{:S(2)}) copy-start(bf16[1,4,192,128]{3,2,1,0:T(8,128)(2,1)} %param.15) | copy-start | bytes 589828
  12.3 17.1 %copy-start.6 = (s32[1,4]{1,0:T(1,128)S(1)}, s32[1,4]{1,0:T(1,128)}, u32[]{:S(2)}) copy-start(s32[1,4]{1,0:T(1,128)} %param.16) | copy-start | bytes 52
  12.3 18.2 %copy-start.4 = (s32[1,4,32,1]{2,3,1,0:T(1,128)S(1)}, s32[1,4,32,1]{2,3,1,0:T(1,128)}, u32[]{:S(2)}) copy-start(s32[1,4,32,1]{2,3,1,0:T(1,128)} %param.17) | copy-start | bytes 1540
  12.3 18.4 %copy-start.5 = (f32[1,4,32]{2,1,0:T(4,128)S(1)}, f32[1,4,32]{2,1,0:T(4,128)}, u32[]{:S(2)}) copy-start(f32[1,4,32]{2,1,0:T(4,128)} %param.19) | copy-start | bytes 1540
  12.3 77.2 %all-to-all-start = ((bf16[64,144,128]{2,1,0:T(8,128)(2,1)}), bf16[64,144,128]{2,1,0:T(8,128)(2,1)S(1)}, u32[]{:S(2)}, u32[]{:S(2)}) async-start(bf16[64,144,128]{2,1,0:T(8,128)(2,1)} %broadcast_in_dim.87), calls=%async_computation | async-start | bytes 4718592 | tf_op jit(solution)/shard_map/all_to_all | solution.py:126
  29.1 2.2 %copy-start.1 = (bf16[1,16,192,128]{3,2,1,0:T(8,128)(2,1)S(1)}, bf16[1,16,192,128]{3,2,1,0:T(8,128)(2,1)}, u32[]{:S(2)}) copy-start(bf16[1,16,192,128]{3,2,1,0:T(8,128)(2,1)} %param.13) | copy-start | bytes 2359300
  29.1 32.0 %all-gather.3.cloned.1.call-start = ((), (), s32[]{:S(2)}) async-start(), calls=%async_computation.2 | async-start | bytes 1806336 | tf_op jit(solution)/shard_map/all_gather | solution.py:112
  89.5 5.5 %copy-start = (bf16[64,144,128]{2,1,0:T(8,128)(2,1)}, bf16[64,144,128]{2,1,0:T(8,128)(2,1)S(1)}, u32[]{:S(2)}) copy-start(bf16[64,144,128]{2,1,0:T(8,128)(2,1)S(1)} %all-to-all-done.g_ref) | copy-start | bytes 7077892
  113.5 18.3 %all-to-all-start.1 = ((f32[64,1,4]{2,1,0:T(1,128)}), f32[64,1,4]{2,1,0:T(1,128)S(1)}, u32[]{:S(2)}, u32[]{:S(2)}) async-start(f32[64,1,4]{2,1,0:T(1,128)} %copy.48), calls=%async_computation.1 | async-start | bytes 65536 | tf_op jit(solution)/shard_map/all_to_all | solution.py:183
Sparse Core Ops, SparseCore 0:
  32.0 29.0 all-gather.2

commit v3 on v2

--- a/solution.py
+++ b/solution.py
@@ -1,4 +1,5 @@
 import functools
+import math
 
 import jax
 import jax.numpy as jnp
@@ -91,6 +92,106 @@
     )(lengths, query_rows, gathered_docs)
 
 
+def exchange_kernel(x_ref, g_ref, ring_send, ring_recv, up_send, up_recv, dn_send, dn_recv, own_sem, *, side):
+    mesh_ids = pl.DeviceIdType.MESH
+    dp = lax.axis_index("dp")
+    odd = lax.axis_index("blk") % 2
+    high, low = dp // side, dp % side
+    p1 = odd * high + (1 - odd) * low
+    p2 = odd * low + (1 - odd) * high
+
+    def dp_of(q1, q2):
+        return odd * (q1 * side + q2) + (1 - odd) * (q2 * side + q1)
+
+    ring_peers = [dp_of((p1 + d) % side, p2) for d in range(1, side)]
+    up_peer = dp_of(p1, (p2 + 1) % side)
+    dn_peer = dp_of(p1, (p2 + side - 1) % side)
+
+    barrier = pltpu.get_barrier_semaphore()
+    for peer in ring_peers + [up_peer, dn_peer]:
+        pl.semaphore_signal(barrier, inc=1, device_id={"dp": peer}, device_id_type=mesh_ids)
+    pl.semaphore_wait(barrier, len(ring_peers) + 2)
+
+    my_slot = p2 * side + p1
+    own = pltpu.make_async_copy(x_ref, g_ref.at[my_slot], own_sem)
+    own.start()
+    ring = []
+    for d in range(1, side):
+        copy = pltpu.make_async_remote_copy(
+            src_ref=x_ref,
+            dst_ref=g_ref.at[my_slot],
+            send_sem=ring_send.at[d - 1],
+            recv_sem=ring_recv.at[d - 1],
+            device_id={"dp": ring_peers[d - 1]},
+            device_id_type=mesh_ids,
+        )
+        copy.start()
+        ring.append(copy)
+    for copy in ring:
+        copy.wait_recv()
+    own.wait()
+
+    def row(r):
+        return g_ref.at[pl.ds(pl.multiple_of(r * side, side), side)]
+
+    ups, dns = [], []
+    up_steps, dn_steps = side // 2, (side - 1) // 2
+    for t in range(max(up_steps, dn_steps)):
+        if t < up_steps:
+            if t > 0:
+                ups[t - 1].wait_recv()
+            r = (p2 + side - t) % side
+            copy = pltpu.make_async_remote_copy(
+                src_ref=row(r),
+                dst_ref=row(r),
+                send_sem=up_send.at[t],
+                recv_sem=up_recv.at[t],
+                device_id={"dp": up_peer},
+                device_id_type=mesh_ids,
+            )
+            copy.start()
+            ups.append(copy)
+        if t < dn_steps:
+            if t > 0:
+                dns[t - 1].wait_recv()
+            r = (p2 + t) % side
+            copy = pltpu.make_async_remote_copy(
+                src_ref=row(r),
+                dst_ref=row(r),
+                send_sem=dn_send.at[t],
+                recv_sem=dn_recv.at[t],
+                device_id={"dp": dn_peer},
+                device_id_type=mesh_ids,
+            )
+            copy.start()
+            dns.append(copy)
+    ups[-1].wait_recv()
+    dns[-1].wait_recv()
+    for copy in ring + ups + dns:
+        copy.wait_send()
+
+
+def gather_plane(block, side):
+    rows, dim = block.shape
+    count = side * side
+    return pl.pallas_call(
+        functools.partial(exchange_kernel, side=side),
+        out_shape=jax.ShapeDtypeStruct((count, rows, dim), block.dtype),
+        in_specs=[pl.BlockSpec(memory_space=pltpu.VMEM)],
+        out_specs=pl.BlockSpec(memory_space=pltpu.VMEM),
+        scratch_shapes=[
+            pltpu.SemaphoreType.DMA((side - 1,)),
+            pltpu.SemaphoreType.DMA((side - 1,)),
+            pltpu.SemaphoreType.DMA((side // 2,)),
+            pltpu.SemaphoreType.DMA((side // 2,)),
+            pltpu.SemaphoreType.DMA(((side - 1) // 2,)),
+            pltpu.SemaphoreType.DMA(((side - 1) // 2,)),
+            pltpu.SemaphoreType.DMA(()),
+        ],
+        compiler_params=pltpu.CompilerParams(collective_id=0, has_side_effects=True),
+    )(block)
+
+
 def per_device(
     queries, passages, passage_lengths, positives, positive_lengths, owners, local_ids, teacher
 ):
@@ -123,13 +224,11 @@
     id_rows = id_rows.reshape(2 * pairs // dim, dim)
     id_block = jnp.zeros((16, dim), jnp.bfloat16).at[: id_rows.shape[0]].set(id_rows)
     send = jnp.concatenate([query_unit, id_block], axis=0)
-    gathered = lax.all_to_all(
-        jnp.broadcast_to(send[None], (peer_count,) + send.shape),
-        "dp",
-        split_axis=0,
-        concat_axis=0,
-        tiled=True,
-    )
+    side = math.isqrt(peer_count)
+    gathered = gather_plane(send, side)
+    slot_index = jnp.arange(peer_count, dtype=jnp.int32)
+    odd = lax.axis_index("blk") % 2
+    slot_of_source = jnp.where(odd == 1, (slot_index % side) * side + slot_index // side, slot_index)
 
     raw_cross = cross_scores(doc_lengths, query_unit, column_docs, query_count, plen)
     logits = jnp.sum(raw_cross.reshape(groups * query_count, query_count, qlen), axis=-1).T
@@ -180,6 +279,7 @@
     group_score = jnp.sum(raw.reshape(group_cap * slots, qlen), axis=-1)
     slot_score = jnp.take(group_score, jnp.minimum(slot_target, group_cap * slots - 1))
     slot_score = jnp.where(slot_valid, slot_score, 0.0).reshape(peer_count, slots)
+    slot_score = jnp.take(slot_score, slot_of_source, axis=0)
     returned = lax.all_to_all(slot_score, "dp", split_axis=0, concat_axis=0, tiled=True)
 
     my_owner = jnp.clip(owners[0, :, :, 0].reshape(pairs), 0, peer_count - 1)

time: 142 us -> 123 us (0.87)
  waiting for transfers between devices: 61.9 us -> 11.2 us
  Pallas kernels: 17.4 us -> 58.7 us
  starting transfers between devices: 23.1 us -> 9.54 us
  other arithmetic: 13.1 us -> 18 us
  local copies, waits for them, and re-layouts: 11.9 us -> 9.63 us
    pallas_call x0 -> x1, Pallas kernels: none -> 46 us  [gather_plane(): pl.pallas_call(functools.partial(exchange_kernel, side=side), out_shape=j...]
    all_gather x1, waiting for transfers between devices: 27.8 us -> 0.01 us  [per_device(): column_docs = lax.all_gather(doc_block, 'blk', axis=0)]
    all_to_all x1 -> x0, waiting for transfers between devices: 22.6 us -> none  [per_device(): lax.all_to_all(jnp.broadcast_to(send[None], (peer_count,) + send.shape),...]
    all_to_all x1 -> x0, starting transfers between devices: 16.7 us -> none  [per_device(): lax.all_to_all(jnp.broadcast_to(send[None], (peer_count,) + send.shape),...]
    pallas_call x1, Pallas kernels: 14.6 us -> 9.88 us  [student_scores(): pl.pallas_call(student_kernel, out_shape=jax.ShapeDtypeStruct((group_cap,...]
    all_to_all x1, starting transfers between devices: 6.31 us -> 9.51 us  [per_device(): lax.all_to_all(slot_score, 'dp', split_axis=0, concat_axis=0, tiled=True)]
    broadcast_in_dim x1 -> x0, local copies, waits for them, and re-layouts: 1.74 us -> none  [per_device(): jnp.broadcast_to(send[None], (peer_count,) + send.shape)]
  transfers between devices with their start and end apart: 3 -> 2, of which waited for: 3 -> 1; matrix products, arithmetic and copies ran while one was open for 5% -> 17% of each run, Pallas kernels for 2% -> 46%
where the time goes in v3:
time: 123 us; the launch traced here: 121 us
  Pallas kernels  58.7 us (48%)
  other arithmetic  18 us (15%)
  between operations  14.4 us (12%)
  waiting for transfers between devices  11.2 us (9%)
  local copies, waits for them, and re-layouts  9.63 us (8%)
  starting transfers between devices  9.54 us (8%)
    pallas_call x1, Pallas kernels, gather_plane(): pl.pallas_call(functools.partial(exchange_kernel, side=side), out_shape=j...  46 us
    all_to_all x1, waiting for transfers between devices, per_device(): lax.all_to_all(slot_score, 'dp', split_axis=0, concat_axis=0, tiled=True)  11.1 us
    pallas_call x1, Pallas kernels, student_scores(): pl.pallas_call(student_kernel, out_shape=jax.ShapeDtypeStruct((group_cap,...  9.88 us
    all_to_all x1, starting transfers between devices, per_device(): lax.all_to_all(slot_score, 'dp', split_axis=0, concat_axis=0, tiled=True)  9.51 us
    convert_element_type x3, other arithmetic, unit_rows(): return (wide * lax.rsqrt(total)).astype(jnp.bfloat16)  3.29 us
    pallas_call x1, Pallas kernels, cross_scores(): pl.pallas_call(functools.partial(cross_kernel, plen=plen), out_shape=jax....  2.85 us
    reduce_sum x3, other arithmetic, unit_rows(): total = jnp.sum(wide * wide, axis=-1, keepdims=True) + 1e-06  2.61 us
  transfers between devices with their start and end apart: 2, of which 1 were waited for; matrix products, arithmetic and copies ran while one was open for 17% of the time, Pallas kernels for 46%

profile of v3, /device:TPU:6, one launch (start us, length us, event | category | flops | bytes accessed | tf_op | source)
XLA Modules:
  0.0 121.5 jit_solution(2725219244763916152)
XLA Ops:
  7.2 0.7 convert_element_type.85
  7.9 1.1 multiply_reduce_fusion
  9.1 1.1 fusion.3
  10.2 0.7 fusion.4
  10.9 0.7 clamp_convert_fusion
  11.6 0.1 min.65
  11.7 0.7 convert_reduce_fusion.1
  12.4 0.1 min.62
  12.5 0.8 multiply_reduce_fusion.1
  13.4 0.8 fusion.5.q_ref
  14.3 0.6 pad_maximum_fusion.x_ref
  14.9 46.0 %shard_map.103.g_ref = bf16[64,144,128]{2,1,0:T(8,128)(2,1)} custom-call(bf16[144,128]{1,0:T(8,128)(2,1)} %pad_maximum_fusion.x_ref), custom_call_target="tpu_custom_call" | custom-call | tf_op jit(solution)/shard_map/pallas_call | solution.py:177
  60.9 0.9 slice_convert_fusion
  61.9 0.3 reduce_window_sum.44
  62.2 0.2 select_reduce_fusion.10
  62.5 0.1 copy.41
  62.6 0.1 eq.96
  62.7 0.1 eq.100
  62.8 0.1 reduce_or.39
  62.9 0.1 reduce_or.38
  63.0 0.1 reduce_or.37
  63.2 0.1 reduce_or.36
  63.3 0.1 copy.49
  63.4 0.1 and.171
  63.5 0.1 and.176
  63.6 0.1 reshape.600
  63.8 0.1 convert_reduce_fusion
  63.9 0.1 copy.42
  64.0 0.1 reduce.7
  64.2 0.6 reduce_sum.233
  64.8 0.6 reduce-window.18
  65.4 0.2 slice_reduce_fusion
  65.6 0.1 copy.47
  65.7 0.1 stack.69
  65.8 0.1 broadcast_in_dim.96
  66.0 0.6 fusion
  66.6 1.4 %fusion.1.p_ref = bf16[16,192,128]{2,1,0:T(8,128)(2,1)} fusion(bf16[1,16,192,128]{3,2,1,0:T(8,128)(2,1)S(1)} %copy-done, f32[16,192]{1,0:T(8,128)S(1)} %add_rsqrt_fusion), kind=kLoop, calls=%fused_computation.7 | loop fusion | flops 1179648 | bytes 1585152 | tf_op jit(solution)/shard_map/convert_element_type | solution.py:17
  68.0 0.1 select_reduce_fusion.11
  68.1 0.8 select_reduce_fusion
  68.9 0.6 select_reduce_fusion.12.gpid_ref
  69.5 9.9 %shard_map.104 = f32[80,128]{1,0:T(8,128)} custom-call(s32[1]{0:T(128)} %bitcast.13.n_ref, s32[80]{0:T(128)} %select_reduce_fusion.12.gpid_ref, s32[320]{0:T(512)} %get-tuple-element.38.gsrc_ref, s32[320]{0:T(512)} %get-tuple-element.37.grow_ref, s32[16]{0:T(128)} %bitcast.105, bf16[64,144,128]{2,1,0:T(8,128)(2,1)} %shard_map.103.g_ref, ...), custom_call_target="tpu_custom_call" | custom-call | flops 503316480 | bytes 3186688 | tf_op jit(solution)/shard_map/pallas_call | solution.py:47
  79.3 0.9 reshape.599
  80.2 0.1 add.293
  80.4 0.1 reduce_sum.242
  80.5 1.9 %gather_fusion = f32[256]{0:T(256)S(1)} fusion(f32[320]{0:T(512)S(1)} %reduce_sum.242, s32[1024]{0:T(1024)S(1)} %pad_clamp_fusion.1), kind=kCustom, calls=%fused_computation | custom fusion | bytes 3072 | tf_op jit(solution)/shard_map/jit(_take)/gather | solution.py:280
  82.5 0.1 gather.22
  82.7 0.6 gather_fusion.1
  83.3 0.7 bitcast_select_fusion
  84.0 9.5 %all-to-all-start = ((f32[64,1,4]{2,1,0:T(1,128)}), f32[64,1,4]{2,1,0:T(1,128)S(1)}, u32[]{:S(2)}, u32[]{:S(2)}) async-start(f32[64,1,4]{2,1,0:T(1,128)} %bitcast.25), calls=%async_computation | async-start | bytes 65536 | tf_op jit(solution)/shard_map/all_to_all | solution.py:283
  93.7 0.2 reduce_window_sum.47
  94.0 0.2 select_reduce_fusion.2
  94.2 0.1 fusion.17
  94.3 11.1 %all-to-all-done = f32[64,1,4]{2,1,0:T(1,128)S(1)} async-done(((f32[64,1,4]{2,1,0:T(1,128)}), f32[64,1,4]{2,1,0:T(1,128)S(1)}, u32[]{:S(2)}, u32[]{:S(2)}) %all-to-all-start) | async-done | bytes 1056 | tf_op jit(solution)/shard_map/all_to_all | solution.py:283
  105.5 1.3 %gather_fusion.2 = f32[128]{0:T(128)S(1)} fusion(f32[64,4]{1,0:T(8,128)S(1)} %bitcast.85, s32[128]{0:T(128)S(1)} %fusion.29), kind=kCustom, calls=%fused_computation.2 | custom fusion | bytes 2048 | tf_op jit(solution)/shard_map/gather | solution.py:290
  106.7 0.7 broadcast_in_dim_reshape.2
  107.5 0.1 exponential_reduce_fusion.1
  107.6 0.7 multiply_reduce_fusion.2
  108.3 0.7 fusion.16
  109.1 0.6 reshape.607.len_ref
  109.7 2.9 %shard_map.105 = f32[32,128]{1,0:T(8,128)} custom-call(s32[32]{0:T(128)} %reshape.607.len_ref, bf16[128,128]{1,0:T(8,128)(2,1)} %copy-done.1, bf16[8,784,128]{2,1,0:T(8,128)(2,1)} %bitcast.87), custom_call_target="tpu_custom_call" | custom-call | flops 205520896 | bytes 1654784 | tf_op jit(solution)/shard_map/pallas_call | solution.py:81
  112.5 0.8 reshape.602
  113.3 0.1 reduce_sum.248
  113.5 0.6 gather_fusion.3
  114.1 0.5 fusion.22
  (49 shorter events, 1.0 us)
Async XLA Ops:
  7.2 101.2 %all-gather.3.cloned.1.call-start = ((), (), s32[]{:S(2)}) async-start(), calls=%async_computation.1 | async-start | bytes 1806336 | tf_op jit(solution)/shard_map/all_gather | solution.py:213
  14.3 48.7 %copy-start.1 = (bf16[128,128]{1,0:T(8,128)(2,1)}, bf16[128,128]{1,0:T(8,128)(2,1)S(1)}, u32[]{:S(2)}) copy-start(bf16[128,128]{1,0:T(8,128)(2,1)S(1)} %fusion.5.q_ref) | copy-start | bytes 98308
  14.9 51.0 %copy-start = (bf16[1,16,192,128]{3,2,1,0:T(8,128)(2,1)S(1)}, bf16[1,16,192,128]{3,2,1,0:T(8,128)(2,1)}, u32[]{:S(2)}) copy-start(bf16[1,16,192,128]{3,2,1,0:T(8,128)(2,1)} %param.13) | copy-start | bytes 2359300
  79.3 14.1 %copy-start.2 = (s32[1,4,32,1]{2,3,1,0:T(1,128)S(1)}, s32[1,4,32,1]{2,3,1,0:T(1,128)}, u32[]{:S(2)}) copy-start(s32[1,4,32,1]{2,3,1,0:T(1,128)} %param.17) | copy-start | bytes 1540
  79.3 14.8 %copy-start.3 = (f32[1,4,32]{2,1,0:T(4,128)S(1)}, f32[1,4,32]{2,1,0:T(4,128)}, u32[]{:S(2)}) copy-start(f32[1,4,32]{2,1,0:T(4,128)} %param.19) | copy-start | bytes 1540
  84.0 21.5 %all-to-all-start = ((f32[64,1,4]{2,1,0:T(1,128)}), f32[64,1,4]{2,1,0:T(1,128)S(1)}, u32[]{:S(2)}, u32[]{:S(2)}) async-start(f32[64,1,4]{2,1,0:T(1,128)} %bitcast.25), calls=%async_computation | async-start | bytes 65536 | tf_op jit(solution)/shard_map/all_to_all | solution.py:283
Sparse Core Ops, SparseCore 0:
  11.0 32.9 all-gather.2

commit v4 on v3

--- a/solution.py
+++ b/solution.py
@@ -92,7 +92,10 @@
     )(lengths, query_rows, gathered_docs)
 
 
-def exchange_kernel(x_ref, g_ref, ring_send, ring_recv, up_send, up_recv, dn_send, dn_recv, own_sem, *, side):
+def exchange_kernel(
+    x_ref, d_ref, g_ref, e_ref, ring_send, ring_recv, up_send, up_recv, dn_send, dn_recv,
+    blk_send, blk_recv, own_sem, doc_sem, *, side
+):
     mesh_ids = pl.DeviceIdType.MESH
     dp = lax.axis_index("dp")
     odd = lax.axis_index("blk") % 2
@@ -107,10 +110,31 @@
     up_peer = dp_of(p1, (p2 + 1) % side)
     dn_peer = dp_of(p1, (p2 + side - 1) % side)
 
+    groups = e_ref.shape[0]
+    me_blk = lax.axis_index("blk")
+    blk_peers = [(me_blk + e) % groups for e in range(1, groups)]
+
     barrier = pltpu.get_barrier_semaphore()
     for peer in ring_peers + [up_peer, dn_peer]:
         pl.semaphore_signal(barrier, inc=1, device_id={"dp": peer}, device_id_type=mesh_ids)
-    pl.semaphore_wait(barrier, len(ring_peers) + 2)
+    for peer in blk_peers:
+        pl.semaphore_signal(barrier, inc=1, device_id={"blk": peer}, device_id_type=mesh_ids)
+    pl.semaphore_wait(barrier, len(ring_peers) + 2 + len(blk_peers))
+
+    docs = []
+    for e in range(1, groups):
+        copy = pltpu.make_async_remote_copy(
+            src_ref=d_ref,
+            dst_ref=e_ref.at[me_blk],
+            send_sem=blk_send.at[e - 1],
+            recv_sem=blk_recv.at[e - 1],
+            device_id={"blk": blk_peers[e - 1]},
+            device_id_type=mesh_ids,
+        )
+        copy.start()
+        docs.append(copy)
+    own_doc = pltpu.make_async_copy(d_ref, e_ref.at[me_blk], doc_sem)
+    own_doc.start()
 
     my_slot = p2 * side + p1
     own = pltpu.make_async_copy(x_ref, g_ref.at[my_slot], own_sem)
@@ -167,18 +191,24 @@
             dns.append(copy)
     ups[-1].wait_recv()
     dns[-1].wait_recv()
-    for copy in ring + ups + dns:
+    for copy in docs:
+        copy.wait_recv()
+    own_doc.wait()
+    for copy in ring + ups + dns + docs:
         copy.wait_send()
 
 
-def gather_plane(block, side):
+def gather_plane(block, doc_block, side, groups):
     rows, dim = block.shape
     count = side * side
     return pl.pallas_call(
         functools.partial(exchange_kernel, side=side),
-        out_shape=jax.ShapeDtypeStruct((count, rows, dim), block.dtype),
-        in_specs=[pl.BlockSpec(memory_space=pltpu.VMEM)],
-        out_specs=pl.BlockSpec(memory_space=pltpu.VMEM),
+        out_shape=(
+            jax.ShapeDtypeStruct((count, rows, dim), block.dtype),
+            jax.ShapeDtypeStruct((groups,) + doc_block.shape, doc_block.dtype),
+        ),
+        in_specs=[pl.BlockSpec(memory_space=pltpu.VMEM)] * 2,
+        out_specs=(pl.BlockSpec(memory_space=pltpu.VMEM),) * 2,
         scratch_shapes=[
             pltpu.SemaphoreType.DMA((side - 1,)),
             pltpu.SemaphoreType.DMA((side - 1,)),
@@ -186,10 +216,72 @@
             pltpu.SemaphoreType.DMA((side // 2,)),
             pltpu.SemaphoreType.DMA(((side - 1) // 2,)),
             pltpu.SemaphoreType.DMA(((side - 1) // 2,)),
+            pltpu.SemaphoreType.DMA((groups - 1,)),
+            pltpu.SemaphoreType.DMA((groups - 1,)),
+            pltpu.SemaphoreType.DMA(()),
             pltpu.SemaphoreType.DMA(()),
         ],
         compiler_params=pltpu.CompilerParams(collective_id=0, has_side_effects=True),
-    )(block)
+    )(block, doc_block)
+
+
+def return_kernel(x_ref, o_ref, send_sems, recv_sems, own_sem):
+    mesh_ids = pl.DeviceIdType.MESH
+    count = x_ref.shape[0]
+    me = lax.axis_index("dp")
+    barrier = pltpu.get_barrier_semaphore()
+
+    def signal(d, carry):
+        pl.semaphore_signal(
+            barrier, inc=1, device_id={"dp": (me + d) % count}, device_id_type=mesh_ids
+        )
+        return carry
+
+    lax.fori_loop(1, count, signal, 0)
+    pl.semaphore_wait(barrier, count - 1)
+    own = pltpu.make_async_copy(x_ref.at[me], o_ref.at[me], own_sem)
+    own.start()
+
+    def describe(d):
+        target = (me + d) % count
+        return pltpu.make_async_remote_copy(
+            src_ref=x_ref.at[target],
+            dst_ref=o_ref.at[me],
+            send_sem=send_sems.at[d - 1],
+            recv_sem=recv_sems.at[d - 1],
+            device_id={"dp": target},
+            device_id_type=mesh_ids,
+        )
+
+    def start(d, carry):
+        describe(d).start()
+        return carry
+
+    def finish(d, carry):
+        copy = describe(d)
+        copy.wait_recv()
+        copy.wait_send()
+        return carry
+
+    lax.fori_loop(1, count, start, 0)
+    own.wait()
+    lax.fori_loop(1, count, finish, 0)
+
+
+def return_scores(rows):
+    count = rows.shape[0]
+    return pl.pallas_call(
+        return_kernel,
+        out_shape=jax.ShapeDtypeStruct(rows.shape, rows.dtype),
+        in_specs=[pl.BlockSpec(memory_space=pltpu.VMEM)],
+        out_specs=pl.BlockSpec(memory_space=pltpu.VMEM),
+        scratch_shapes=[
+            pltpu.SemaphoreType.DMA((count - 1,)),
+            pltpu.SemaphoreType.DMA((count - 1,)),
+            pltpu.SemaphoreType.DMA(()),
+        ],
+        compiler_params=pltpu.CompilerParams(collective_id=1, has_side_effects=True),
+    )(rows)
 
 
 def per_device(
@@ -210,9 +302,6 @@
         positive_lengths[0].astype(jnp.bfloat16)
     )
     doc_block = jnp.concatenate([positive_unit, length_row], axis=0)
-    column_docs = lax.all_gather(doc_block, "blk", axis=0)
-    groups = column_docs.shape[0]
-    doc_lengths = column_docs[:, query_count * plen, :query_count].astype(jnp.int32).reshape(-1)
 
     query_unit = unit_rows(queries[0]).reshape(query_count * qlen, dim)
     id_rows = jnp.stack(
@@ -225,7 +314,9 @@
     id_block = jnp.zeros((16, dim), jnp.bfloat16).at[: id_rows.shape[0]].set(id_rows)
     send = jnp.concatenate([query_unit, id_block], axis=0)
     side = math.isqrt(peer_count)
-    gathered = gather_plane(send, side)
+    groups = lax.axis_size("blk")
+    gathered, column_docs = gather_plane(send, doc_block, side, groups)
+    doc_lengths = column_docs[:, query_count * plen, :query_count].astype(jnp.int32).reshape(-1)
     slot_index = jnp.arange(peer_count, dtype=jnp.int32)
     odd = lax.axis_index("blk") % 2
     slot_of_source = jnp.where(odd == 1, (slot_index % side) * side + slot_index // side, slot_index)
@@ -280,7 +371,8 @@
     slot_score = jnp.take(group_score, jnp.minimum(slot_target, group_cap * slots - 1))
     slot_score = jnp.where(slot_valid, slot_score, 0.0).reshape(peer_count, slots)
     slot_score = jnp.take(slot_score, slot_of_source, axis=0)
-    returned = lax.all_to_all(slot_score, "dp", split_axis=0, concat_axis=0, tiled=True)
+    padded = jnp.zeros((peer_count, 8, 128), jnp.float32).at[:, 0, :slots].set(slot_score)
+    returned = return_scores(padded)[:, 0, :slots]
 
     my_owner = jnp.clip(owners[0, :, :, 0].reshape(pairs), 0, peer_count - 1)
     owner_hot = (my_owner[:, None] == jnp.arange(peer_count, dtype=jnp.int32)[None, :]).astype(

time: 123 us -> 112 us (0.911)
  Pallas kernels: 58.7 us -> 80.6 us
  between operations: 14.4 us -> 1.06 us
  waiting for transfers between devices: 11.2 us -> 0 us
  starting transfers between devices: 9.54 us -> 0 us
  local copies, waits for them, and re-layouts: 9.63 us -> 11.3 us
    pallas_call x1 -> x2, Pallas kernels: 46 us -> 67.6 us  [the longest x1 46.9 us: gather_plane(): pl.pallas_call(functools.partial(exchange_kernel, side=side), out_shape=(...]
    all_to_all x1 -> x0, waiting for transfers between devices: 11.1 us -> none  [per_device(): lax.all_to_all(slot_score, 'dp', split_axis=0, concat_axis=0, tiled=True)]
    all_to_all x1 -> x0, starting transfers between devices: 9.51 us -> none  [per_device(): lax.all_to_all(slot_score, 'dp', split_axis=0, concat_axis=0, tiled=True)]
  transfers between devices with their start and end apart: 2 -> 0, of which waited for: 1 -> 0; matrix products, arithmetic and copies ran while one was open for 17% -> 0% of each run, Pallas kernels for 46% -> 0%
where the time goes in v4:
time: 112 us; the launch traced here: 110 us
  Pallas kernels  80.6 us (72%)
  other arithmetic  17.6 us (16%)
  local copies, waits for them, and re-layouts  11.3 us (10%)
    pallas_call x1, Pallas kernels, gather_plane(): pl.pallas_call(functools.partial(exchange_kernel, side=side), out_shape=(...  46.9 us
    pallas_call x1, Pallas kernels, return_scores(): pl.pallas_call(return_kernel, out_shape=jax.ShapeDtypeStruct(rows.shape,...  20.7 us
    pallas_call x1, Pallas kernels, student_scores(): pl.pallas_call(student_kernel, out_shape=jax.ShapeDtypeStruct((group_cap,...  10.1 us
    convert_element_type x3, other arithmetic, unit_rows(): return (wide * lax.rsqrt(total)).astype(jnp.bfloat16)  3.29 us
    pallas_call x1, Pallas kernels, cross_scores(): pl.pallas_call(functools.partial(cross_kernel, plen=plen), out_shape=jax....  2.85 us
    reduce_sum x3, other arithmetic, unit_rows(): total = jnp.sum(wide * wide, axis=-1, keepdims=True) + 1e-06  2.61 us
    another operation x6, other arithmetic  2.25 us

profile of v4, /device:TPU:6, one launch (start us, length us, event | category | flops | bytes accessed | tf_op | source)
XLA Modules:
  0.0 110.5 jit_solution(13603403846380931473)
XLA Ops:
  0.6 0.8 clamp_convert_fusion
  1.4 0.1 min.65
  1.5 0.7 convert_reduce_fusion.2
  2.2 0.1 min.62
  2.3 0.8 multiply_reduce_fusion.1
  3.2 0.8 fusion.5.q_ref
  4.1 0.6 pad_maximum_fusion.x_ref
  4.7 0.7 convert_element_type.76
  5.4 1.1 %multiply_reduce_fusion = f32[4,192]{1,0:T(4,128)S(1)} fusion(bf16[1,4,192,128]{3,2,1,0:T(8,128)(2,1)} %param.17), kind=kLoop, calls=%fused_computation.12 | loop fusion | flops 294144 | bytes 199680 | tf_op jit(solution)/shard_map/reduce_sum | solution.py:16
  6.6 1.1 fusion.3
  7.7 0.7 fusion.4.d_ref
  8.4 46.9 %shard_map.103 = (bf16[64,144,128]{2,1,0:T(8,128)(2,1)}, bf16[8,784,128]{2,1,0:T(8,128)(2,1)}) custom-call(bf16[144,128]{1,0:T(8,128)(2,1)} %pad_maximum_fusion.x_ref, bf16[784,128]{1,0:T(8,128)(2,1)} %fusion.4.d_ref), custom_call_target="tpu_custom_call" | custom-call | tf_op jit(solution)/shard_map/pallas_call | solution.py:204
  55.4 0.9 slice_convert_fusion
  56.4 0.3 reduce_window_sum.44
  56.7 0.2 select_reduce_fusion.10
  56.9 0.1 reduce_or.39
  57.0 0.1 reduce_or.38
  57.1 0.1 reduce_or.37
  57.3 0.1 reduce_or.36
  57.4 0.1 copy.48
  57.5 0.1 copy.40
  57.6 0.1 eq.96
  57.7 0.1 and.174
  57.9 0.1 convert_reduce_fusion
  58.1 0.1 reduce.9
  58.3 0.6 reduce_sum.234
  58.9 0.6 select_reduce_fusion.12.gpid_ref
  59.5 0.1 eq.100
  59.6 0.1 and.179
  59.7 0.6 reduce-window.18
  60.3 0.2 slice_reduce_fusion
  60.5 0.1 select_reduce_fusion.11
  60.7 0.1 copy.46
  60.8 0.1 stack.69
  60.9 0.1 broadcast_in_dim.97
  61.0 0.8 select_reduce_fusion
  61.8 0.6 fusion
  62.4 1.4 %fusion.1.p_ref = bf16[16,192,128]{2,1,0:T(8,128)(2,1)} fusion(bf16[1,16,192,128]{3,2,1,0:T(8,128)(2,1)S(1)} %copy-done, f32[16,192]{1,0:T(8,128)S(1)} %add_rsqrt_fusion), kind=kLoop, calls=%fused_computation.7 | loop fusion | flops 1179648 | bytes 1585152 | tf_op jit(solution)/shard_map/convert_element_type | solution.py:17
  63.8 10.1 %shard_map.104 = f32[80,128]{1,0:T(8,128)} custom-call(s32[1]{0:T(128)} %bitcast.14.n_ref, s32[80]{0:T(128)} %select_reduce_fusion.12.gpid_ref, s32[320]{0:T(512)} %get-tuple-element.54.gsrc_ref, s32[320]{0:T(512)} %get-tuple-element.53.grow_ref, s32[16]{0:T(128)} %bitcast.101, bf16[64,144,128]{2,1,0:T(8,128)(2,1)} %get-tuple-element.41.g_ref, ...), custom_call_target="tpu_custom_call" | custom-call | flops 503316480 | bytes 3186688 | tf_op jit(solution)/shard_map/pallas_call | solution.py:47
  73.9 0.9 reshape.626
  74.7 0.1 reduce_sum.243
  74.9 0.1 reshape.627
  75.1 1.9 %gather_fusion = f32[256]{0:T(256)S(1)} fusion(f32[320]{0:T(512)S(1)} %reduce_sum.243, s32[1024]{0:T(1024)S(1)} %pad_clamp_fusion.1), kind=kCustom, calls=%fused_computation | custom fusion | bytes 3072 | tf_op jit(solution)/shard_map/jit(_take)/gather | solution.py:371
  77.0 0.1 gather.22
  77.1 0.1 add.299
  77.3 0.6 gather_fusion.1
  77.9 0.1 broadcast_select_fusion
  78.0 0.7 scatter.14.x_ref
  78.8 20.7 %shard_map.105 = f32[64,8,128]{2,1,0:T(8,128)} custom-call(f32[64,8,128]{2,1,0:T(8,128)} %scatter.14.x_ref), custom_call_target="tpu_custom_call" | custom-call | tf_op jit(solution)/shard_map/pallas_call | solution.py:273
  99.5 1.0 slice.81
  100.7 0.2 reduce_window_sum.47
  100.8 0.2 select_reduce_fusion.2
  101.1 1.3 %gather_fusion.2 = f32[128]{0:T(128)S(1)} fusion(f32[64,4]{1,0:T(8,128)S(1)} %bitcast.82, s32[128]{0:T(128)S(1)} %fusion.28), kind=kCustom, calls=%fused_computation.2 | custom fusion | bytes 2048 | tf_op jit(solution)/shard_map/gather | solution.py:382
  102.4 0.7 broadcast_in_dim_reshape.2
  103.1 0.1 exponential_reduce_fusion.1
  103.3 0.1 fusion.16
  103.4 0.7 multiply_reduce_fusion.2
  104.1 0.7 convert_reduce_fusion.1
  104.8 0.6 reshape.634.len_ref
  105.4 2.9 %shard_map.106 = f32[32,128]{1,0:T(8,128)} custom-call(s32[32]{0:T(128)} %reshape.634.len_ref, bf16[128,128]{1,0:T(8,128)(2,1)} %copy-done.1, bf16[8,784,128]{2,1,0:T(8,128)(2,1)} %get-tuple-element.42.p_ref), custom_call_target="tpu_custom_call" | custom-call | flops 205520896 | bytes 1654784 | tf_op jit(solution)/shard_map/pallas_call | solution.py:81
  108.3 0.8 reshape.629
  109.1 0.1 reduce_sum.248
  109.3 0.6 gather_fusion.3
  109.9 0.5 fusion.21
  (47 shorter events, 1.0 us)
Async XLA Ops:
  0.6 61.2 %copy-start = (bf16[1,16,192,128]{3,2,1,0:T(8,128)(2,1)S(1)}, bf16[1,16,192,128]{3,2,1,0:T(8,128)(2,1)}, u32[]{:S(2)}) copy-start(bf16[1,16,192,128]{3,2,1,0:T(8,128)(2,1)} %param.15) | copy-start | bytes 2359300
  4.1 58.3 %copy-start.1 = (bf16[128,128]{1,0:T(8,128)(2,1)}, bf16[128,128]{1,0:T(8,128)(2,1)S(1)}, u32[]{:S(2)}) copy-start(bf16[128,128]{1,0:T(8,128)(2,1)S(1)} %fusion.5.q_ref) | copy-start | bytes 98308
  73.9 26.6 %copy-start.2 = (s32[1,4,32,1]{2,3,1,0:T(1,128)S(1)}, s32[1,4,32,1]{2,3,1,0:T(1,128)}, u32[]{:S(2)}) copy-start(s32[1,4,32,1]{2,3,1,0:T(1,128)} %param.19) | copy-start | bytes 1540
  75.0 28.2 %copy-start.3 = (f32[1,4,32]{2,1,0:T(4,128)S(1)}, f32[1,4,32]{2,1,0:T(4,128)}, u32[]{:S(2)}) copy-start(f32[1,4,32]{2,1,0:T(4,128)} %param.21) | copy-start | bytes 1540

commit v5 on v4

--- a/solution.py
+++ b/solution.py
@@ -9,12 +9,6 @@
 from jax.sharding import PartitionSpec as P
 
 NEG = -1000000000.0
-
-
-def unit_rows(values):
-    wide = values.astype(jnp.float32)
-    total = jnp.sum(wide * wide, axis=-1, keepdims=True) + 1e-06
-    return (wide * lax.rsqrt(total)).astype(jnp.bfloat16)
 
 
 def student_kernel(n_ref, gpid_ref, gsrc_ref, grow_ref, len_ref, g_ref, p_ref, o_ref):
@@ -58,43 +52,17 @@
     )(n_groups, gpid, gsrc, grow, lengths, gathered, passage_unit)
 
 
-def cross_kernel(len_ref, q_ref, p_ref, o_ref, *, plen):
-    groups = p_ref.shape[0]
-    docs = o_ref.shape[0] // groups
-    row_ids = lax.broadcasted_iota(jnp.int32, (plen, q_ref.shape[0]), 0)
-    q = q_ref[...]
-    for e in range(groups):
-        for k in range(docs):
-            sim = lax.dot_general(
-                p_ref[e, k * plen : (k + 1) * plen, :],
-                q,
-                (((1,), (1,)), ((), ())),
-                preferred_element_type=jnp.float32,
-            )
-            sim = jnp.where(row_ids < len_ref[e * docs + k], sim, NEG)
-            o_ref[pl.ds(e * docs + k, 1), :] = jnp.max(sim, axis=0, keepdims=True)
-
-
-def cross_scores(lengths, query_rows, gathered_docs, doc_count, plen):
-    groups, rows, dim = gathered_docs.shape
-    cols = query_rows.shape[0]
-    return pl.pallas_call(
-        functools.partial(cross_kernel, plen=plen),
-        out_shape=jax.ShapeDtypeStruct((groups * doc_count, cols), jnp.float32),
-        in_specs=[pl.BlockSpec(memory_space=pltpu.SMEM)]
-        + [pl.BlockSpec(memory_space=pltpu.VMEM)] * 2,
-        out_specs=pl.BlockSpec(memory_space=pltpu.VMEM),
-        cost_estimate=pl.CostEstimate(
-            flops=2 * groups * rows * dim * cols,
-            transcendentals=0,
-            bytes_accessed=query_rows.size * 2 + gathered_docs.size * 2 + groups * doc_count * cols * 4,
-        ),
-    )(lengths, query_rows, gathered_docs)
+def unit_block(values):
+    wide = values.astype(jnp.float32)
+    total = jnp.sum(wide * wide, axis=-1, keepdims=True) + 1e-06
+    return (wide * lax.rsqrt(total)).astype(jnp.bfloat16)
 
 
 def exchange_kernel(
-    x_ref, d_ref, g_ref, e_ref, ring_send, ring_recv, up_send, up_recv, dn_send, dn_recv,
-    blk_send, blk_recv, own_sem, doc_sem, *, side
+    q_ref, id_ref, pos_ref, lrow_ref, pas_ref,
+    g_ref, e_ref, pu_ref, c_ref,
+    x_buf, d_buf, ring_send, ring_recv, up_send, up_recv, dn_send, dn_recv,
+    blk_send, blk_recv, own_sem, doc_sem, *, side, plen
 ):
     mesh_ids = pl.DeviceIdType.MESH
     dp = lax.axis_index("dp")
@@ -109,7 +77,6 @@
     ring_peers = [dp_of((p1 + d) % side, p2) for d in range(1, side)]
     up_peer = dp_of(p1, (p2 + 1) % side)
     dn_peer = dp_of(p1, (p2 + side - 1) % side)
-
     groups = e_ref.shape[0]
     me_blk = lax.axis_index("blk")
     blk_peers = [(me_blk + e) % groups for e in range(1, groups)]
@@ -119,12 +86,18 @@
         pl.semaphore_signal(barrier, inc=1, device_id={"dp": peer}, device_id_type=mesh_ids)
     for peer in blk_peers:
         pl.semaphore_signal(barrier, inc=1, device_id={"blk": peer}, device_id_type=mesh_ids)
+
+    nq, npos = q_ref.shape[0], pos_ref.shape[0]
+    x_buf[0:nq, :] = unit_block(q_ref[...])
+    x_buf[nq:, :] = id_ref[...]
+    d_buf[0:npos, :] = unit_block(pos_ref[...])
+    d_buf[npos:, :] = lrow_ref[...]
     pl.semaphore_wait(barrier, len(ring_peers) + 2 + len(blk_peers))
 
     docs = []
     for e in range(1, groups):
         copy = pltpu.make_async_remote_copy(
-            src_ref=d_ref,
+            src_ref=d_buf,
             dst_ref=e_ref.at[me_blk],
             send_sem=blk_send.at[e - 1],
             recv_sem=blk_recv.at[e - 1],
@@ -133,16 +106,16 @@
         )
         copy.start()
         docs.append(copy)
-    own_doc = pltpu.make_async_copy(d_ref, e_ref.at[me_blk], doc_sem)
+    own_doc = pltpu.make_async_copy(d_buf, e_ref.at[me_blk], doc_sem)
     own_doc.start()
 
     my_slot = p2 * side + p1
-    own = pltpu.make_async_copy(x_ref, g_ref.at[my_slot], own_sem)
+    own = pltpu.make_async_copy(x_buf, g_ref.at[my_slot], own_sem)
     own.start()
     ring = []
     for d in range(1, side):
         copy = pltpu.make_async_remote_copy(
-            src_ref=x_ref,
+            src_ref=x_buf,
             dst_ref=g_ref.at[my_slot],
             send_sem=ring_send.at[d - 1],
             recv_sem=ring_recv.at[d - 1],
@@ -158,9 +131,35 @@
     def row(r):
         return g_ref.at[pl.ds(pl.multiple_of(r * side, side), side)]
 
+    def normalize_passages():
+        for p in range(pas_ref.shape[0]):
+            pu_ref[p] = unit_block(pas_ref[p])
+
+    def score_positives():
+        for copy in docs:
+            copy.wait_recv()
+        own_doc.wait()
+        docs_per_group = c_ref.shape[0] // groups
+        q = x_buf[0:nq, :]
+        row_ids = lax.broadcasted_iota(jnp.int32, (plen, nq), 0).astype(jnp.float32)
+        lane = lax.broadcasted_iota(jnp.int32, (1, lrow_ref.shape[1]), 1)
+        for e in range(groups):
+            lengths = e_ref[e, npos:, :].astype(jnp.float32)[0:1, :]
+            for k in range(docs_per_group):
+                kept = jnp.sum(jnp.where(lane == k, lengths, 0.0), axis=1, keepdims=True)
+                sim = lax.dot_general(
+                    e_ref[e, k * plen : (k + 1) * plen, :],
+                    q,
+                    (((1,), (1,)), ((), ())),
+                    preferred_element_type=jnp.float32,
+                )
+                sim = jnp.where(row_ids < kept, sim, NEG)
+                c_ref[pl.ds(e * docs_per_group + k, 1), :] = jnp.max(sim, axis=0, keepdims=True)
+
     ups, dns = [], []
     up_steps, dn_steps = side // 2, (side - 1) // 2
-    for t in range(max(up_steps, dn_steps)):
+    steps = max(up_steps, dn_steps)
+    for t in range(steps):
         if t < up_steps:
             if t > 0:
                 ups[t - 1].wait_recv()
@@ -189,27 +188,35 @@
             )
             copy.start()
             dns.append(copy)
+        if t == 0:
+            normalize_passages()
+        if t == min(2, steps - 1):
+            score_positives()
     ups[-1].wait_recv()
     dns[-1].wait_recv()
-    for copy in docs:
-        copy.wait_recv()
-    own_doc.wait()
     for copy in ring + ups + dns + docs:
         copy.wait_send()
 
 
-def gather_plane(block, doc_block, side, groups):
-    rows, dim = block.shape
+def gather_plane(queries, id_block, positives, length_row, passages, side, groups, doc_count):
+    nq, dim = queries.shape
+    rows = nq + id_block.shape[0]
+    doc_rows = positives.shape[0] + length_row.shape[0]
+    plen = passages.shape[1]
     count = side * side
     return pl.pallas_call(
-        functools.partial(exchange_kernel, side=side),
+        functools.partial(exchange_kernel, side=side, plen=plen),
         out_shape=(
-            jax.ShapeDtypeStruct((count, rows, dim), block.dtype),
-            jax.ShapeDtypeStruct((groups,) + doc_block.shape, doc_block.dtype),
+            jax.ShapeDtypeStruct((count, rows, dim), jnp.bfloat16),
+            jax.ShapeDtypeStruct((groups, doc_rows, dim), jnp.bfloat16),
+            jax.ShapeDtypeStruct(passages.shape, jnp.bfloat16),
+            jax.ShapeDtypeStruct((groups * doc_count, nq), jnp.float32),
         ),
-        in_specs=[pl.BlockSpec(memory_space=pltpu.VMEM)] * 2,
-        out_specs=(pl.BlockSpec(memory_space=pltpu.VMEM),) * 2,
+        in_specs=[pl.BlockSpec(memory_space=pltpu.VMEM)] * 5,
+        out_specs=(pl.BlockSpec(memory_space=pltpu.VMEM),) * 4,
         scratch_shapes=[
+            pltpu.VMEM((rows, dim), jnp.bfloat16),
+            pltpu.VMEM((doc_rows, dim), jnp.bfloat16),
             pltpu.SemaphoreType.DMA((side - 1,)),
             pltpu.SemaphoreType.DMA((side - 1,)),
             pltpu.SemaphoreType.DMA((side // 2,)),
@@ -222,7 +229,7 @@
             pltpu.SemaphoreType.DMA(()),
         ],
         compiler_params=pltpu.CompilerParams(collective_id=0, has_side_effects=True),
-    )(block, doc_block)
+    )(queries, id_block, positives, length_row, passages)
 
 
 def return_kernel(x_ref, o_ref, send_sems, recv_sems, own_sem):
@@ -297,13 +304,10 @@
     lanes = slots * qlen
     group_cap = peer_count * slots // slots + pass_count
 
-    positive_unit = unit_rows(positives[0]).reshape(query_count * plen, dim)
+    groups = lax.axis_size("blk")
     length_row = jnp.zeros((16, dim), jnp.bfloat16).at[0, :query_count].set(
         positive_lengths[0].astype(jnp.bfloat16)
     )
-    doc_block = jnp.concatenate([positive_unit, length_row], axis=0)
-
-    query_unit = unit_rows(queries[0]).reshape(query_count * qlen, dim)
     id_rows = jnp.stack(
         [
             jnp.clip(owners[0, :, :, 0].reshape(pairs), 0, peer_count - 1),
@@ -312,16 +316,21 @@
     ).astype(jnp.bfloat16)
     id_rows = id_rows.reshape(2 * pairs // dim, dim)
     id_block = jnp.zeros((16, dim), jnp.bfloat16).at[: id_rows.shape[0]].set(id_rows)
-    send = jnp.concatenate([query_unit, id_block], axis=0)
     side = math.isqrt(peer_count)
-    groups = lax.axis_size("blk")
-    gathered, column_docs = gather_plane(send, doc_block, side, groups)
-    doc_lengths = column_docs[:, query_count * plen, :query_count].astype(jnp.int32).reshape(-1)
+    gathered, column_docs, passage_unit, raw_cross = gather_plane(
+        queries[0].reshape(query_count * qlen, dim),
+        id_block,
+        positives[0].reshape(query_count * plen, dim),
+        length_row,
+        passages[0],
+        side,
+        groups,
+        query_count,
+    )
     slot_index = jnp.arange(peer_count, dtype=jnp.int32)
     odd = lax.axis_index("blk") % 2
     slot_of_source = jnp.where(odd == 1, (slot_index % side) * side + slot_index // side, slot_index)
 
-    raw_cross = cross_scores(doc_lengths, query_unit, column_docs, query_count, plen)
     logits = jnp.sum(raw_cross.reshape(groups * query_count, query_count, qlen), axis=-1).T
     own_column = lax.axis_index("blk") * query_count + jnp.arange(query_count, dtype=jnp.int32)
     own_logit = jnp.take_along_axis(logits, own_column[:, None], axis=1)[:, 0]
@@ -363,7 +372,6 @@
         ),
         axis=1,
     )
-    passage_unit = unit_rows(passages[0])
     raw = student_scores(
         n_groups, gpid, gsrc, grow, passage_lengths[0], gathered, passage_unit, group_cap, lanes
     )

time: 112 us -> 102 us (0.911); the launches traced: 110 us -> 102 us
  other arithmetic: 17.6 us -> 10.1 us
    convert_element_type x4 -> x0, other arithmetic: 4.03 us -> none  [the longest x3 3.29 us: unit_rows(): return (wide * lax.rsqrt(total)).astype(jnp.bfloat16)]
    reduce_sum x3 -> x0, other arithmetic: 2.61 us -> none  [unit_rows(): total = jnp.sum(wide * wide, axis=-1, keepdims=True) + 1e-06]
    pallas_call x2 -> x1, Pallas kernels: 49.8 us -> 47.6 us  [gather_plane(): pl.pallas_call(functools.partial(exchange_kernel, side=side, plen=plen),...]
    pallas_call x1, Pallas kernels: 20.7 us -> 22.7 us  [return_scores(): pl.pallas_call(return_kernel, out_shape=jax.ShapeDtypeStruct(rows.shape,...]
    concatenate x2 -> x0, other arithmetic: 1.31 us -> none  [the longest x1 0.7 us: per_device(): doc_block = jnp.concatenate([positive_unit, length_row], axis=0)]
where the time goes in v5:
time: 102 us
  Pallas kernels  80.2 us (79%)
  local copies, waits for them, and re-layouts  10.4 us (10%)
  other arithmetic  10.1 us (10%)
    pallas_call x1, Pallas kernels, gather_plane(): pl.pallas_call(functools.partial(exchange_kernel, side=side, plen=plen),...  47.6 us
    pallas_call x1, Pallas kernels, return_scores(): pl.pallas_call(return_kernel, out_shape=jax.ShapeDtypeStruct(rows.shape,...  22.7 us
    pallas_call x1, Pallas kernels, student_scores(): pl.pallas_call(student_kernel, out_shape=jax.ShapeDtypeStruct((group_cap,...  9.89 us
    another operation x6, other arithmetic  2.17 us
    gather x2, local copies, waits for them, and re-layouts, per_device(): jnp.take(group_score, jnp.minimum(slot_target, group_cap * slots - 1))  2.05 us

profile of v5, /device:TPU:6, one launch (start us, length us, event | category | flops | bytes accessed | tf_op | source)
XLA Modules:
  0.0 101.7 jit_solution(18310819880160203378)
XLA Ops:
  0.6 0.7 convert_reduce_fusion.1
  1.3 0.1 min.62
  1.4 0.7 clamp_convert_fusion
  2.1 0.1 min.65
  2.2 0.6 fusion.9.id_ref
  2.8 0.7 convert_element_type.24
  3.5 0.6 scatter.11.lrow_ref
  4.1 47.6 %shard_map.103 = (bf16[64,144,128]{2,1,0:T(8,128)(2,1)}, bf16[8,784,128]{2,1,0:T(8,128)(2,1)}, bf16[16,192,128]{2,1,0:T(8,128)(2,1)}, f32[32,128]{1,0:T(8,128)}) custom-call(bf16[128,128]{1,0:T(8,128)(2,1)} %bitcast.79, bf16[16,128]{1,0:T(8,128)(2,1)} %fusion.9.id_ref, bf16[768,128]{1,0:T(8,128)(2,1)} %bitcast.75, bf16[16,128]{1,0:T(8,128)(2,1)} %scatter.11.lrow_ref, ...), custom_call_target="tpu_custom_call" | custom-call | tf_op jit(solution)/shard_map/pallas_call | solution.py:207
  51.6 0.9 slice_convert_fusion
  52.6 0.1 fusion.25
  52.7 0.3 reduce_window_sum.44
  53.0 0.2 select_reduce_fusion.10
  53.2 0.1 reduce_or.36
  53.3 0.1 reduce_or.37
  53.4 0.1 reduce_or.38
  53.5 0.1 reduce_or.39
  53.7 0.1 copy.48
  53.8 0.1 and.179
  53.9 0.1 copy.40
  54.0 0.1 eq.100
  54.1 0.6 reduce-window.18
  54.7 0.2 slice_reduce_fusion
  55.0 0.1 and.174
  55.1 0.1 eq.96
  55.2 0.1 convert_reduce_fusion
  55.3 0.1 copy.41
  55.5 0.1 reduce.7
  55.6 0.1 select_reduce_fusion.11
  55.7 0.1 copy.46
  55.8 0.1 stack.69
  55.9 0.1 reshape.579
  56.1 0.1 broadcast_in_dim.94
  56.2 0.8 select_reduce_fusion
  57.0 0.6 select_reduce_fusion.12.gpid_ref
  57.6 0.6 reduce_sum.205
  58.2 9.9 %shard_map.104 = f32[80,128]{1,0:T(8,128)} custom-call(s32[1]{0:T(128)} %bitcast.15.n_ref, s32[80]{0:T(128)} %select_reduce_fusion.12.gpid_ref, s32[320]{0:T(512)} %get-tuple-element.56.gsrc_ref, s32[320]{0:T(512)} %get-tuple-element.55.grow_ref, s32[16]{0:T(128)} %bitcast.95, bf16[64,144,128]{2,1,0:T(8,128)(2,1)} %get-tuple-element.42.g_ref, ...), custom_call_target="tpu_custom_call" | custom-call | flops 503316480 | bytes 3186688 | tf_op jit(solution)/shard_map/pallas_call | solution.py:41
  68.1 0.9 reshape.578
  69.0 0.1 reduce_sum.213
  69.1 2.0 %gather_fusion = f32[256]{0:T(256)S(1)} fusion(f32[320]{0:T(512)S(1)} %reduce_sum.213, s32[1024]{0:T(1024)S(1)} %pad_clamp_fusion.1), kind=kCustom, calls=%fused_computation | custom fusion | bytes 3072 | tf_op jit(solution)/shard_map/jit(_take)/gather | solution.py:379
  71.1 0.1 gather.22
  71.2 0.1 add.260
  71.4 0.6 gather_fusion.1
  72.0 0.1 broadcast_select_fusion
  72.1 0.7 scatter.14.x_ref
  72.9 22.7 %shard_map.105 = f32[64,8,128]{2,1,0:T(8,128)} custom-call(f32[64,8,128]{2,1,0:T(8,128)} %scatter.14.x_ref), custom_call_target="tpu_custom_call" | custom-call | tf_op jit(solution)/shard_map/pallas_call | solution.py:280
  95.6 1.0 slice.78
  96.6 0.0 copy-done.1
  96.6 0.1 min.71
  96.7 0.1 fusion
  96.8 0.2 reduce_window_sum.47
  97.0 0.2 select_reduce_fusion.2
  97.1 0.1 min.70
  97.2 1.3 %gather_fusion.2 = f32[128]{0:T(128)S(1)} fusion(f32[64,4]{1,0:T(8,128)S(1)} %bitcast.73, s32[128]{0:T(128)S(1)} %fusion.22), kind=kCustom, calls=%fused_computation.2 | custom fusion | bytes 2048 | tf_op jit(solution)/shard_map/gather | solution.py:390
  98.5 0.1 reshape.580
  98.6 0.1 exponential_reduce_fusion.1
  98.7 0.0 copy-done.2
  98.7 0.1 fusion.10
  98.9 0.7 multiply_reduce_fusion
  99.6 0.7 broadcast_in_dim_reshape.2
  100.3 0.0 copy-done
  100.3 0.1 reshape.581
  100.4 0.1 reduce_sum.218
  100.5 0.6 gather_fusion.3
  101.2 0.5 fusion.15
  (30 shorter events, 0.4 us)
Async XLA Ops:
  58.2 38.4 %copy-start.1 = (s32[1,4,32,1]{2,3,1,0:T(1,128)S(1)}, s32[1,4,32,1]{2,3,1,0:T(1,128)}, u32[]{:S(2)}) copy-start(s32[1,4,32,1]{2,3,1,0:T(1,128)} %param.19) | copy-start | bytes 1540
  68.1 30.6 %copy-start.2 = (f32[1,4,32]{2,1,0:T(4,128)S(1)}, f32[1,4,32]{2,1,0:T(4,128)}, u32[]{:S(2)}) copy-start(f32[1,4,32]{2,1,0:T(4,128)} %param.21) | copy-start | bytes 1540
  68.1 32.2 %copy-start = (f32[32,128]{1,0:T(8,128)S(1)}, f32[32,128]{1,0:T(8,128)}, u32[]{:S(2)}) copy-start(f32[32,128]{1,0:T(8,128)} %get-tuple-element.44) | copy-start | bytes 49156

commit v6 on v5

--- a/solution.py
+++ b/solution.py
@@ -108,28 +108,6 @@
         docs.append(copy)
     own_doc = pltpu.make_async_copy(d_buf, e_ref.at[me_blk], doc_sem)
     own_doc.start()
-
-    my_slot = p2 * side + p1
-    own = pltpu.make_async_copy(x_buf, g_ref.at[my_slot], own_sem)
-    own.start()
-    ring = []
-    for d in range(1, side):
-        copy = pltpu.make_async_remote_copy(
-            src_ref=x_buf,
-            dst_ref=g_ref.at[my_slot],
-            send_sem=ring_send.at[d - 1],
-            recv_sem=ring_recv.at[d - 1],
-            device_id={"dp": ring_peers[d - 1]},
-            device_id_type=mesh_ids,
-        )
-        copy.start()
-        ring.append(copy)
-    for copy in ring:
-        copy.wait_recv()
-    own.wait()
-
-    def row(r):
-        return g_ref.at[pl.ds(pl.multiple_of(r * side, side), side)]
 
     def normalize_passages():
         for p in range(pas_ref.shape[0]):
@@ -156,45 +134,62 @@
                 sim = jnp.where(row_ids < kept, sim, NEG)
                 c_ref[pl.ds(e * docs_per_group + k, 1), :] = jnp.max(sim, axis=0, keepdims=True)
 
-    ups, dns = [], []
+    my_slot = p2 * side + p1
+    own = pltpu.make_async_copy(x_buf, g_ref.at[my_slot], own_sem)
+    own.start()
+    ring = []
+    for d in range(1, side):
+        copy = pltpu.make_async_remote_copy(
+            src_ref=x_buf,
+            dst_ref=g_ref.at[my_slot],
+            send_sem=ring_send.at[d - 1],
+            recv_sem=ring_recv.at[d - 1],
+            device_id={"dp": ring_peers[d - 1]},
+            device_id_type=mesh_ids,
+        )
+        copy.start()
+        ring.append(copy)
+    normalize_passages()
+    for copy in ring:
+        copy.wait_recv()
+    own.wait()
+
+    chunks = up_send.shape[1]
+    width = side // chunks
     up_steps, dn_steps = side // 2, (side - 1) // 2
     steps = max(up_steps, dn_steps)
+
+    def forward(t, c, peer, r, sends, recvs):
+        part = pl.ds(pl.multiple_of(r * side + c * width, width), width)
+        copy = pltpu.make_async_remote_copy(
+            src_ref=g_ref.at[part],
+            dst_ref=g_ref.at[part],
+            send_sem=sends.at[t, c],
+            recv_sem=recvs.at[t, c],
+            device_id={"dp": peer},
+            device_id_type=mesh_ids,
+        )
+        copy.start()
+        return copy
+
+    ups, dns = [], []
     for t in range(steps):
-        if t < up_steps:
-            if t > 0:
-                ups[t - 1].wait_recv()
-            r = (p2 + side - t) % side
-            copy = pltpu.make_async_remote_copy(
-                src_ref=row(r),
-                dst_ref=row(r),
-                send_sem=up_send.at[t],
-                recv_sem=up_recv.at[t],
-                device_id={"dp": up_peer},
-                device_id_type=mesh_ids,
-            )
-            copy.start()
-            ups.append(copy)
-        if t < dn_steps:
-            if t > 0:
-                dns[t - 1].wait_recv()
-            r = (p2 + t) % side
-            copy = pltpu.make_async_remote_copy(
-                src_ref=row(r),
-                dst_ref=row(r),
-                send_sem=dn_send.at[t],
-                recv_sem=dn_recv.at[t],
-                device_id={"dp": dn_peer},
-                device_id_type=mesh_ids,
-            )
-            copy.start()
-            dns.append(copy)
-        if t == 0:
-            normalize_passages()
-        if t == min(2, steps - 1):
-            score_positives()
-    ups[-1].wait_recv()
-    dns[-1].wait_recv()
-    for copy in ring + ups + dns + docs:
+        ups.append([])
+        dns.append([])
+        for c in range(chunks):
+            if t < up_steps:
+                if t > 0:
+                    ups[t - 1][c].wait_recv()
+                ups[t].append(forward(t, c, up_peer, (p2 + side - t) % side, up_send, up_recv))
+            if t < dn_steps:
+                if t > 0:
+                    dns[t - 1][c].wait_recv()
+                dns[t].append(forward(t, c, dn_peer, (p2 + t) % side, dn_send, dn_recv))
+    score_positives()
+    for copy in ups[up_steps - 1] + dns[dn_steps - 1]:
+        copy.wait_recv()
+    sent = [copy for step in ups + dns for copy in step]
+    for copy in ring + sent + docs:
         copy.wait_send()
 
 
@@ -204,6 +199,7 @@
     doc_rows = positives.shape[0] + length_row.shape[0]
     plen = passages.shape[1]
     count = side * side
+    chunks = math.gcd(side, 4)
     return pl.pallas_call(
         functools.partial(exchange_kernel, side=side, plen=plen),
         out_shape=(
@@ -219,10 +215,10 @@
             pltpu.VMEM((doc_rows, dim), jnp.bfloat16),
             pltpu.SemaphoreType.DMA((side - 1,)),
             pltpu.SemaphoreType.DMA((side - 1,)),
-            pltpu.SemaphoreType.DMA((side // 2,)),
-            pltpu.SemaphoreType.DMA((side // 2,)),
-            pltpu.SemaphoreType.DMA(((side - 1) // 2,)),
-            pltpu.SemaphoreType.DMA(((side - 1) // 2,)),
+            pltpu.SemaphoreType.DMA((side // 2, chunks)),
+            pltpu.SemaphoreType.DMA((side // 2, chunks)),
+            pltpu.SemaphoreType.DMA(((side - 1) // 2, chunks)),
+            pltpu.SemaphoreType.DMA(((side - 1) // 2, chunks)),
             pltpu.SemaphoreType.DMA((groups - 1,)),
             pltpu.SemaphoreType.DMA((groups - 1,)),
             pltpu.SemaphoreType.DMA(()),

time: 102 us -> 96 us (0.941)
  Pallas kernels: 80.2 us -> 74.2 us
    pallas_call x1, Pallas kernels: 47.6 us -> 40.9 us  [gather_plane(): pl.pallas_call(functools.partial(exchange_kernel, side=side, plen=plen),...]
where the time goes in v6:
time: 96 us; the launch traced here: 95.6 us
  Pallas kernels  74.2 us (77%)
  local copies, waits for them, and re-layouts  10.4 us (11%)
  other arithmetic  10.1 us (11%)
    pallas_call x1, Pallas kernels, gather_plane(): pl.pallas_call(functools.partial(exchange_kernel, side=side, plen=plen),...  40.9 us
    pallas_call x1, Pallas kernels, return_scores(): pl.pallas_call(return_kernel, out_shape=jax.ShapeDtypeStruct(rows.shape,...  23.7 us
    pallas_call x1, Pallas kernels, student_scores(): pl.pallas_call(student_kernel, out_shape=jax.ShapeDtypeStruct((group_cap,...  9.54 us
    another operation x6, other arithmetic  2.17 us
    gather x2, local copies, waits for them, and re-layouts, per_device(): jnp.take(group_score, jnp.minimum(slot_target, group_cap * slots - 1))  2.05 us

profile of v6, /device:TPU:6, one launch (start us, length us, event | category | flops | bytes accessed | tf_op | source)
XLA Modules:
  0.0 95.6 jit_solution(13262486268147073977)
XLA Ops:
  0.6 0.7 convert_reduce_fusion.1
  1.3 0.1 min.62
  1.4 0.7 clamp_convert_fusion
  2.1 0.1 min.65
  2.2 0.6 fusion.9.id_ref
  2.8 0.7 convert_element_type.24
  3.5 0.6 scatter.11.lrow_ref
  4.1 40.9 %shard_map.103 = (bf16[64,144,128]{2,1,0:T(8,128)(2,1)}, bf16[8,784,128]{2,1,0:T(8,128)(2,1)}, bf16[16,192,128]{2,1,0:T(8,128)(2,1)}, f32[32,128]{1,0:T(8,128)}) custom-call(bf16[128,128]{1,0:T(8,128)(2,1)} %bitcast.79, bf16[16,128]{1,0:T(8,128)(2,1)} %fusion.9.id_ref, bf16[768,128]{1,0:T(8,128)(2,1)} %bitcast.75, bf16[16,128]{1,0:T(8,128)(2,1)} %scatter.11.lrow_ref, ...), custom_call_target="tpu_custom_call" | custom-call | tf_op jit(solution)/shard_map/pallas_call | solution.py:203
  44.9 0.9 slice_convert_fusion
  45.9 0.1 fusion.25
  46.0 0.3 reduce_window_sum.44
  46.3 0.2 select_reduce_fusion.10
  46.5 0.1 reduce_or.36
  46.6 0.1 reduce_or.37
  46.7 0.1 reduce_or.38
  46.8 0.1 reduce_or.39
  47.0 0.1 copy.48
  47.1 0.1 and.179
  47.2 0.1 copy.40
  47.3 0.1 eq.100
  47.5 0.6 reduce-window.18
  48.0 0.2 slice_reduce_fusion
  48.3 0.1 and.174
  48.4 0.1 eq.96
  48.5 0.1 convert_reduce_fusion
  48.6 0.1 copy.41
  48.8 0.1 reduce.7
  48.9 0.1 select_reduce_fusion.11
  49.0 0.1 copy.46
  49.1 0.1 stack.69
  49.2 0.1 reshape.579
  49.4 0.1 broadcast_in_dim.94
  49.5 0.8 select_reduce_fusion
  50.3 0.6 select_reduce_fusion.12.gpid_ref
  50.9 0.6 reduce_sum.205
  51.5 9.5 %shard_map.104 = f32[80,128]{1,0:T(8,128)} custom-call(s32[1]{0:T(128)} %bitcast.15.n_ref, s32[80]{0:T(128)} %select_reduce_fusion.12.gpid_ref, s32[320]{0:T(512)} %get-tuple-element.56.gsrc_ref, s32[320]{0:T(512)} %get-tuple-element.55.grow_ref, s32[16]{0:T(128)} %bitcast.95, bf16[64,144,128]{2,1,0:T(8,128)(2,1)} %get-tuple-element.42.g_ref, ...), custom_call_target="tpu_custom_call" | custom-call | flops 503316480 | bytes 3186688 | tf_op jit(solution)/shard_map/pallas_call | solution.py:41
  61.1 0.9 reshape.578
  61.9 0.1 reduce_sum.213
  62.1 2.0 %gather_fusion = f32[256]{0:T(256)S(1)} fusion(f32[320]{0:T(512)S(1)} %reduce_sum.213, s32[1024]{0:T(1024)S(1)} %pad_clamp_fusion.1), kind=kCustom, calls=%fused_computation | custom fusion | bytes 3072 | tf_op jit(solution)/shard_map/jit(_take)/gather | solution.py:375
  64.1 0.1 gather.22
  64.2 0.1 add.260
  64.3 0.6 gather_fusion.1
  65.0 0.1 broadcast_select_fusion
  65.1 0.7 scatter.14.x_ref
  65.8 23.7 %shard_map.105 = f32[64,8,128]{2,1,0:T(8,128)} custom-call(f32[64,8,128]{2,1,0:T(8,128)} %scatter.14.x_ref), custom_call_target="tpu_custom_call" | custom-call | tf_op jit(solution)/shard_map/pallas_call | solution.py:276
  89.6 1.0 %slice.78 = f32[64,1,4]{2,1,0:T(1,128)S(1)} slice(f32[64,8,128]{2,1,0:T(8,128)} %shard_map.105), slice={[0:64], [0:1], [0:4]} | slice | bytes 2048 | tf_op jit(solution)/shard_map/slice | solution.py:379
  90.5 0.0 copy-done.1
  90.6 0.1 min.71
  90.6 0.1 fusion
  90.7 0.2 reduce_window_sum.47
  90.9 0.2 select_reduce_fusion.2
  91.1 0.1 min.70
  91.2 1.3 %gather_fusion.2 = f32[128]{0:T(128)S(1)} fusion(f32[64,4]{1,0:T(8,128)S(1)} %bitcast.73, s32[128]{0:T(128)S(1)} %fusion.22), kind=kCustom, calls=%fused_computation.2 | custom fusion | bytes 2048 | tf_op jit(solution)/shard_map/gather | solution.py:386
  92.5 0.1 reshape.580
  92.6 0.1 exponential_reduce_fusion.1
  92.7 0.0 copy-done.2
  92.7 0.1 fusion.10
  92.8 0.7 multiply_reduce_fusion
  93.5 0.7 broadcast_in_dim_reshape.2
  94.2 0.0 copy-done
  94.2 0.1 reshape.581
  94.3 0.1 reduce_sum.218
  94.5 0.6 gather_fusion.3
  95.1 0.5 fusion.15
  (30 shorter events, 0.4 us)
Async XLA Ops:
  51.5 39.0 %copy-start.1 = (s32[1,4,32,1]{2,3,1,0:T(1,128)S(1)}, s32[1,4,32,1]{2,3,1,0:T(1,128)}, u32[]{:S(2)}) copy-start(s32[1,4,32,1]{2,3,1,0:T(1,128)} %param.19) | copy-start | bytes 1540
  61.0 31.6 %copy-start.2 = (f32[1,4,32]{2,1,0:T(4,128)S(1)}, f32[1,4,32]{2,1,0:T(4,128)}, u32[]{:S(2)}) copy-start(f32[1,4,32]{2,1,0:T(4,128)} %param.21) | copy-start | bytes 1540
  61.0 33.2 %copy-start = (f32[32,128]{1,0:T(8,128)S(1)}, f32[32,128]{1,0:T(8,128)}, u32[]{:S(2)}) copy-start(f32[32,128]{1,0:T(8,128)} %get-tuple-element.44) | copy-start | bytes 49156

commit v7 on v6

--- a/solution.py
+++ b/solution.py
@@ -9,47 +9,6 @@
 from jax.sharding import PartitionSpec as P
 
 NEG = -1000000000.0
-
-
-def student_kernel(n_ref, gpid_ref, gsrc_ref, grow_ref, len_ref, g_ref, p_ref, o_ref):
-    lanes = o_ref.shape[1]
-    slots = gsrc_ref.shape[0] // o_ref.shape[0]
-    qlen = lanes // slots
-    plen = p_ref.shape[1]
-    row_ids = lax.broadcasted_iota(jnp.int32, (plen, lanes), 0)
-
-    def body(g, carry):
-        pieces = []
-        for r in range(slots):
-            src = gsrc_ref[g * slots + r]
-            j = grow_ref[g * slots + r]
-            pieces.append(g_ref[src, pl.ds(pl.multiple_of(j * qlen, qlen), qlen), :])
-        q = jnp.concatenate(pieces, axis=0)
-        pidx = gpid_ref[g]
-        sim = lax.dot_general(
-            p_ref[pidx], q, (((1,), (1,)), ((), ())), preferred_element_type=jnp.float32
-        )
-        sim = jnp.where(row_ids < len_ref[pidx], sim, NEG)
-        o_ref[pl.ds(g, 1), :] = jnp.max(sim, axis=0, keepdims=True)
-        return carry
-
-    lax.fori_loop(0, n_ref[0], body, 0)
-
-
-def student_scores(n_groups, gpid, gsrc, grow, lengths, gathered, passage_unit, group_cap, lanes):
-    plen, dim = passage_unit.shape[1], passage_unit.shape[2]
-    return pl.pallas_call(
-        student_kernel,
-        out_shape=jax.ShapeDtypeStruct((group_cap, lanes), jnp.float32),
-        in_specs=[pl.BlockSpec(memory_space=pltpu.SMEM)] * 5
-        + [pl.BlockSpec(memory_space=pltpu.VMEM)] * 2,
-        out_specs=pl.BlockSpec(memory_space=pltpu.VMEM),
-        cost_estimate=pl.CostEstimate(
-            flops=2 * group_cap * plen * dim * lanes,
-            transcendentals=0,
-            bytes_accessed=gathered.size * 2 + passage_unit.size * 2 + group_cap * lanes * 4,
-        ),
-    )(n_groups, gpid, gsrc, grow, lengths, gathered, passage_unit)
 
 
 def unit_block(values):
@@ -228,10 +187,16 @@
     )(queries, id_block, positives, length_row, passages)
 
 
-def return_kernel(x_ref, o_ref, send_sems, recv_sems, own_sem):
+def score_return_kernel(
+    pid_ref, len_ref, g_ref, p_ref, o_ref, x_buf, send_sems, recv_sems, own_sem, *, side
+):
     mesh_ids = pl.DeviceIdType.MESH
-    count = x_ref.shape[0]
+    count = g_ref.shape[0]
+    slots = pid_ref.shape[0] // count
+    lanes = o_ref.shape[2]
+    plen = p_ref.shape[1]
     me = lax.axis_index("dp")
+    odd = lax.axis_index("blk") % 2
     barrier = pltpu.get_barrier_semaphore()
 
     def signal(d, carry):
@@ -241,14 +206,33 @@
         return carry
 
     lax.fori_loop(1, count, signal, 0)
+    x_buf[...] = jnp.zeros(x_buf.shape, jnp.float32)
+    row_ids = lax.broadcasted_iota(jnp.int32, (plen, lanes), 0)
+
+    def body(s, carry):
+        q = g_ref[s, 0:lanes, :]
+        for r in range(slots):
+            pidx = pid_ref[s * slots + r]
+            sim = lax.dot_general(
+                p_ref[pidx], q, (((1,), (1,)), ((), ())), preferred_element_type=jnp.float32
+            )
+            sim = jnp.where(row_ids < len_ref[pidx], sim, NEG)
+            x_buf[s, pl.ds(r, 1), :] = jnp.max(sim, axis=0, keepdims=True)
+        return carry
+
+    lax.fori_loop(0, count, body, 0)
     pl.semaphore_wait(barrier, count - 1)
-    own = pltpu.make_async_copy(x_ref.at[me], o_ref.at[me], own_sem)
+
+    def slot_of(t):
+        return odd * ((t % side) * side + t // side) + (1 - odd) * t
+
+    own = pltpu.make_async_copy(x_buf.at[slot_of(me)], o_ref.at[me], own_sem)
     own.start()
 
     def describe(d):
         target = (me + d) % count
         return pltpu.make_async_remote_copy(
-            src_ref=x_ref.at[target],
+            src_ref=x_buf.at[slot_of(target)],
             dst_ref=o_ref.at[me],
             send_sem=send_sems.at[d - 1],
             recv_sem=recv_sems.at[d - 1],
@@ -271,20 +255,29 @@
     lax.fori_loop(1, count, finish, 0)
 
 
-def return_scores(rows):
-    count = rows.shape[0]
+def score_and_return(pid, lengths, gathered, passage_unit, side, lanes):
+    count = gathered.shape[0]
+    plen, dim = passage_unit.shape[1], passage_unit.shape[2]
+    slots = pid.shape[0] // count
     return pl.pallas_call(
-        return_kernel,
-        out_shape=jax.ShapeDtypeStruct(rows.shape, rows.dtype),
-        in_specs=[pl.BlockSpec(memory_space=pltpu.VMEM)],
+        functools.partial(score_return_kernel, side=side),
+        out_shape=jax.ShapeDtypeStruct((count, 8, lanes), jnp.float32),
+        in_specs=[pl.BlockSpec(memory_space=pltpu.SMEM)] * 2
+        + [pl.BlockSpec(memory_space=pltpu.VMEM)] * 2,
         out_specs=pl.BlockSpec(memory_space=pltpu.VMEM),
         scratch_shapes=[
+            pltpu.VMEM((count, 8, lanes), jnp.float32),
             pltpu.SemaphoreType.DMA((count - 1,)),
             pltpu.SemaphoreType.DMA((count - 1,)),
             pltpu.SemaphoreType.DMA(()),
         ],
+        cost_estimate=pl.CostEstimate(
+            flops=2 * count * slots * plen * dim * lanes,
+            transcendentals=0,
+            bytes_accessed=gathered.size * 2 + passage_unit.size * 2,
+        ),
         compiler_params=pltpu.CompilerParams(collective_id=1, has_side_effects=True),
-    )(rows)
+    )(pid, lengths, gathered, passage_unit)
 
 
 def per_device(
@@ -298,7 +291,6 @@
     pairs = query_count * cand_count
     slots = 4
     lanes = slots * qlen
-    group_cap = peer_count * slots // slots + pass_count
 
     groups = lax.axis_size("blk")
     length_row = jnp.zeros((16, dim), jnp.bfloat16).at[0, :query_count].set(
@@ -323,9 +315,6 @@
         groups,
         query_count,
     )
-    slot_index = jnp.arange(peer_count, dtype=jnp.int32)
-    odd = lax.axis_index("blk") % 2
-    slot_of_source = jnp.where(odd == 1, (slot_index % side) * side + slot_index // side, slot_index)
 
     logits = jnp.sum(raw_cross.reshape(groups * query_count, query_count, qlen), axis=-1).T
     own_column = lax.axis_index("blk") * query_count + jnp.arange(query_count, dtype=jnp.int32)
@@ -337,53 +326,24 @@
     pair_owner, pair_local = ids[:, 0, :], ids[:, 1, :]
     hit = (pair_owner == me).astype(jnp.int32)
     rank = jnp.cumsum(hit, axis=1) - hit
-    pair_index = lax.broadcasted_iota(jnp.int32, (peer_count, pairs), 1)
     chosen = [(hit > 0) & (rank == r) for r in range(slots)]
-    slot_pair = jnp.stack([jnp.sum(jnp.where(c, pair_index, 0), axis=1) for c in chosen], axis=1)
     slot_local = jnp.stack([jnp.sum(jnp.where(c, pair_local, 0), axis=1) for c in chosen], axis=1)
-    slot_valid = jnp.stack([jnp.any(c, axis=1) for c in chosen], axis=1).reshape(-1)
-    slot_pid = slot_local.reshape(-1)
-    slot_src = (lax.broadcasted_iota(jnp.int32, (peer_count, slots), 0)).reshape(-1)
-    slot_row = (slot_pair // cand_count).reshape(-1)
-
-    by_pass = (
-        slot_valid[:, None] & (slot_pid[:, None] == jnp.arange(pass_count, dtype=jnp.int32)[None, :])
-    ).astype(jnp.int32)
-    per_pass = jnp.sum(by_pass, axis=0)
-    pass_groups = (per_pass + slots - 1) // slots
-    pass_base = jnp.cumsum(pass_groups) - pass_groups
-    n_groups = jnp.sum(pass_groups).reshape(1)
-    in_pass = jnp.sum((jnp.cumsum(by_pass, axis=0) - by_pass) * by_pass, axis=1)
-    slot_target = jnp.sum(pass_base[None, :] * by_pass, axis=1) * slots + in_pass
-    slot_target = jnp.where(slot_valid, slot_target, group_cap * slots)
-    target_hit = slot_target[None, :] == jnp.arange(group_cap * slots, dtype=jnp.int32)[:, None]
-    gsrc = jnp.sum(jnp.where(target_hit, slot_src[None, :], 0), axis=1)
-    grow = jnp.sum(jnp.where(target_hit, slot_row[None, :], 0), axis=1)
-    group_index = jnp.arange(group_cap, dtype=jnp.int32)[:, None]
-    gpid = jnp.sum(
-        jnp.where(
-            (group_index >= pass_base[None, :]) & (group_index < (pass_base + pass_groups)[None, :]),
-            jnp.arange(pass_count, dtype=jnp.int32)[None, :],
-            0,
-        ),
-        axis=1,
-    )
-    raw = student_scores(
-        n_groups, gpid, gsrc, grow, passage_lengths[0], gathered, passage_unit, group_cap, lanes
-    )
-    group_score = jnp.sum(raw.reshape(group_cap * slots, qlen), axis=-1)
-    slot_score = jnp.take(group_score, jnp.minimum(slot_target, group_cap * slots - 1))
-    slot_score = jnp.where(slot_valid, slot_score, 0.0).reshape(peer_count, slots)
-    slot_score = jnp.take(slot_score, slot_of_source, axis=0)
-    padded = jnp.zeros((peer_count, 8, 128), jnp.float32).at[:, 0, :slots].set(slot_score)
-    returned = return_scores(padded)[:, 0, :slots]
+    returned = score_and_return(
+        slot_local.reshape(-1), passage_lengths[0], gathered, passage_unit, side, lanes
+    )
+    per_query = jnp.sum(
+        returned[:, :slots, :].reshape(peer_count, slots, query_count, qlen), axis=-1
+    )
 
     my_owner = jnp.clip(owners[0, :, :, 0].reshape(pairs), 0, peer_count - 1)
     owner_hot = (my_owner[:, None] == jnp.arange(peer_count, dtype=jnp.int32)[None, :]).astype(
         jnp.int32
     )
     my_rank = jnp.sum((jnp.cumsum(owner_hot, axis=0) - owner_hot) * owner_hot, axis=1)
-    student = returned[my_owner, jnp.minimum(my_rank, slots - 1)].reshape(query_count, cand_count)
+    my_query = jnp.arange(pairs, dtype=jnp.int32) // cand_count
+    student = per_query[my_owner, jnp.minimum(my_rank, slots - 1), my_query].reshape(
+        query_count, cand_count
+    )
 
     teacher_score_rows = teacher[0]
     log_teacher = teacher_score_rows - jnp.log(

time: 96 us -> 85.3 us (0.89)
  local copies, waits for them, and re-layouts: 10.4 us -> 5.97 us
  other arithmetic: 10.1 us -> 6.2 us
  Pallas kernels: 74.2 us -> 72.1 us
    reduce_sum x6 -> x1, other arithmetic: 2.37 us -> 0.04 us  [per_device(): jnp.sum(returned[:, :slots, :].reshape(peer_count, slots, query_count, ql...]
    gather x4 -> x1, local copies, waits for them, and re-layouts: 3.93 us -> 1.62 us  [per_device(): per_query[my_owner, jnp.minimum(my_rank, slots - 1), my_query]]
    pallas_call x2 -> x1, Pallas kernels: 33.3 us -> 31.2 us  [score_and_return(): pl.pallas_call(functools.partial(score_return_kernel, side=side), out_sha...]
    another operation x8 -> x2, other arithmetic: 2.2 us -> 1.39 us
where the time goes in v7:
time: 85.3 us; the launch traced here: 85 us
  Pallas kernels  72.1 us (85%)
  other arithmetic  6.2 us (7%)
  local copies, waits for them, and re-layouts  5.97 us (7%)
    pallas_call x1, Pallas kernels, gather_plane(): pl.pallas_call(functools.partial(exchange_kernel, side=side, plen=plen),...  40.9 us
    pallas_call x1, Pallas kernels, score_and_return(): pl.pallas_call(functools.partial(score_return_kernel, side=side), out_sha...  31.2 us

profile of v7, /device:TPU:6, one launch (start us, length us, event | category | flops | bytes accessed | tf_op | source)
XLA Modules:
  0.0 85.0 jit_solution(17113417082775594065)
XLA Ops:
  0.6 0.7 convert_reduce_fusion
  1.3 0.1 min.42
  1.4 0.7 clamp_convert_fusion
  2.1 0.1 min.45
  2.2 0.6 fusion.3.id_ref
  2.8 0.7 convert_element_type.17
  3.5 0.6 scatter.9.lrow_ref
  4.1 40.9 %shard_map.103 = (bf16[64,144,128]{2,1,0:T(8,128)(2,1)}, bf16[8,784,128]{2,1,0:T(8,128)(2,1)}, bf16[16,192,128]{2,1,0:T(8,128)(2,1)}, f32[32,128]{1,0:T(8,128)}) custom-call(bf16[128,128]{1,0:T(8,128)(2,1)} %bitcast.45, bf16[16,128]{1,0:T(8,128)(2,1)} %fusion.3.id_ref, bf16[768,128]{1,0:T(8,128)(2,1)} %bitcast.42, bf16[16,128]{1,0:T(8,128)(2,1)} %scatter.9.lrow_ref, ...), custom_call_target="tpu_custom_call" | custom-call | tf_op jit(solution)/shard_map/pallas_call | solution.py:162
  44.9 0.9 %slice_convert_fusion = s32[64,2,128]{2,1,0:T(2,128)S(1)} fusion(bf16[64,144,128]{2,1,0:T(8,128)(2,1)} %get-tuple-element.30.g_ref), kind=kLoop, calls=%fused_computation.11 | loop fusion | flops 16384 | bytes 98304 | tf_op jit(solution)/shard_map/convert_element_type | solution.py:325
  45.9 0.1 fusion.16
  46.0 0.3 reduce_window_sum.22
  46.3 0.2 select_reduce_fusion.4
  46.4 0.1 copy.20
  46.5 0.7 reshape.280.pid_ref
  47.2 0.0 copy-start.1
  47.2 0.0 copy-start.2
  47.2 0.0 copy-start
  47.2 31.2 %shard_map.104 = f32[64,8,128]{2,1,0:T(8,128)} custom-call(s32[256]{0:T(256)} %reshape.280.pid_ref, s32[16]{0:T(128)} %bitcast.52, bf16[64,144,128]{2,1,0:T(8,128)(2,1)} %get-tuple-element.30.g_ref, bf16[16,192,128]{2,1,0:T(8,128)(2,1)} %get-tuple-element.31.p_ref), custom_call_target="tpu_custom_call" | custom-call | flops 1610612736 | bytes 3145728 | tf_op jit(solution)/shard_map/pallas_call | solution.py:262
  78.4 1.0 %slice.47 = f32[64,4,128]{2,1,0:T(4,128)S(1)} slice(f32[64,8,128]{2,1,0:T(8,128)} %shard_map.104), slice={[0:64], [0:4], [0:128]} | slice | bytes 262144 | tf_op jit(solution)/shard_map/slice | solution.py:335
  79.4 0.1 copy.21
  79.5 0.0 copy-done.1
  79.6 0.1 min.47
  79.7 0.1 fusion
  79.8 0.2 reduce_window_sum.23
  79.9 0.2 select_reduce_fusion
  80.1 0.1 min.46
  80.2 1.6 %gather_fusion = f32[128]{0:T(128)S(1)} fusion(f32[64,4,4]{0,2,1:T(4,128)S(1)} %bitcast_reduce_fusion, s32[128]{0:T(128)S(1)} %fusion.8), kind=kCustom, calls=%fused_computation | custom fusion | bytes 2560 | tf_op jit(solution)/shard_map/gather | solution.py:344
  81.8 0.1 reshape.282
  81.9 0.1 exponential_reduce_fusion.1
  82.1 0.0 copy-done.2
  82.1 0.1 fusion.4
  82.2 0.7 multiply_reduce_fusion
  82.9 0.7 broadcast_in_dim_reshape.3
  83.6 0.0 copy-done
  83.6 0.1 reshape.283
  83.7 0.1 reduce_sum.108
  83.8 0.6 gather_fusion.1
  84.5 0.5 fusion.9
  (12 shorter events, 0.2 us)
Async XLA Ops:
  47.2 32.3 %copy-start.1 = (s32[1,4,32,1]{2,3,1,0:T(1,128)S(1)}, s32[1,4,32,1]{2,3,1,0:T(1,128)}, u32[]{:S(2)}) copy-start(s32[1,4,32,1]{2,3,1,0:T(1,128)} %param.17) | copy-start | bytes 1540
  47.2 34.9 %copy-start.2 = (f32[1,4,32]{2,1,0:T(4,128)S(1)}, f32[1,4,32]{2,1,0:T(4,128)}, u32[]{:S(2)}) copy-start(f32[1,4,32]{2,1,0:T(4,128)} %param.19) | copy-start | bytes 1540
  47.2 36.4 %copy-start = (f32[32,128]{1,0:T(8,128)S(1)}, f32[32,128]{1,0:T(8,128)}, u32[]{:S(2)}) copy-start(f32[32,128]{1,0:T(8,128)} %get-tuple-element.32) | copy-start | bytes 49156

commit v8 on v7

--- a/solution.py
+++ b/solution.py
@@ -158,7 +158,7 @@
     doc_rows = positives.shape[0] + length_row.shape[0]
     plen = passages.shape[1]
     count = side * side
-    chunks = math.gcd(side, 4)
+    chunks = math.gcd(side, 8)
     return pl.pallas_call(
         functools.partial(exchange_kernel, side=side, plen=plen),
         out_shape=(

time: 85.3 us -> 85.5 us (level)
  no operation moved by 1% of the time
where the time goes in v8:
time: 85.5 us; the launch traced here: 85.2 us
  Pallas kernels  72.2 us (84%)
  other arithmetic  6.2 us (7%)
  local copies, waits for them, and re-layouts  5.97 us (7%)
    pallas_call x1, Pallas kernels, gather_plane(): pl.pallas_call(functools.partial(exchange_kernel, side=side, plen=plen),...  40.6 us
    pallas_call x1, Pallas kernels, score_and_return(): pl.pallas_call(functools.partial(score_return_kernel, side=side), out_sha...  31.6 us

profile of v8, /device:TPU:6, one launch (start us, length us, event | category | flops | bytes accessed | tf_op | source)
XLA Modules:
  0.0 85.2 jit_solution(9341851719331726049)
XLA Ops:
  0.6 0.7 convert_reduce_fusion
  1.3 0.1 min.42
  1.4 0.7 clamp_convert_fusion
  2.1 0.1 min.45
  2.2 0.6 fusion.3.id_ref
  2.8 0.7 convert_element_type.17
  3.5 0.6 scatter.9.lrow_ref
  4.1 40.6 %shard_map.103 = (bf16[64,144,128]{2,1,0:T(8,128)(2,1)}, bf16[8,784,128]{2,1,0:T(8,128)(2,1)}, bf16[16,192,128]{2,1,0:T(8,128)(2,1)}, f32[32,128]{1,0:T(8,128)}) custom-call(bf16[128,128]{1,0:T(8,128)(2,1)} %bitcast.45, bf16[16,128]{1,0:T(8,128)(2,1)} %fusion.3.id_ref, bf16[768,128]{1,0:T(8,128)(2,1)} %bitcast.42, bf16[16,128]{1,0:T(8,128)(2,1)} %scatter.9.lrow_ref, ...), custom_call_target="tpu_custom_call" | custom-call | tf_op jit(solution)/shard_map/pallas_call | solution.py:162
  44.6 0.9 %slice_convert_fusion = s32[64,2,128]{2,1,0:T(2,128)S(1)} fusion(bf16[64,144,128]{2,1,0:T(8,128)(2,1)} %get-tuple-element.30.g_ref), kind=kLoop, calls=%fused_computation.11 | loop fusion | flops 16384 | bytes 98304 | tf_op jit(solution)/shard_map/convert_element_type | solution.py:325
  45.6 0.1 fusion.16
  45.6 0.3 reduce_window_sum.22
  45.9 0.2 select_reduce_fusion.4
  46.1 0.1 copy.20
  46.2 0.7 reshape.280.pid_ref
  46.9 0.0 copy-start.1
  46.9 0.0 copy-start.2
  46.9 0.0 copy-start
  46.9 31.6 %shard_map.104 = f32[64,8,128]{2,1,0:T(8,128)} custom-call(s32[256]{0:T(256)} %reshape.280.pid_ref, s32[16]{0:T(128)} %bitcast.52, bf16[64,144,128]{2,1,0:T(8,128)(2,1)} %get-tuple-element.30.g_ref, bf16[16,192,128]{2,1,0:T(8,128)(2,1)} %get-tuple-element.31.p_ref), custom_call_target="tpu_custom_call" | custom-call | flops 1610612736 | bytes 3145728 | tf_op jit(solution)/shard_map/pallas_call | solution.py:262
  78.5 1.0 %slice.47 = f32[64,4,128]{2,1,0:T(4,128)S(1)} slice(f32[64,8,128]{2,1,0:T(8,128)} %shard_map.104), slice={[0:64], [0:4], [0:128]} | slice | bytes 262144 | tf_op jit(solution)/shard_map/slice | solution.py:335
  79.5 0.1 copy.21
  79.7 0.0 copy-done.1
  79.7 0.1 min.47
  79.8 0.1 fusion
  79.9 0.2 reduce_window_sum.23
  80.1 0.2 select_reduce_fusion
  80.3 0.1 min.46
  80.4 1.6 %gather_fusion = f32[128]{0:T(128)S(1)} fusion(f32[64,4,4]{0,2,1:T(4,128)S(1)} %bitcast_reduce_fusion, s32[128]{0:T(128)S(1)} %fusion.8), kind=kCustom, calls=%fused_computation | custom fusion | bytes 2560 | tf_op jit(solution)/shard_map/gather | solution.py:344
  82.0 0.1 reshape.282
  82.1 0.1 exponential_reduce_fusion.1
  82.2 0.0 copy-done.2
  82.2 0.1 fusion.4
  82.3 0.7 multiply_reduce_fusion
  83.1 0.7 broadcast_in_dim_reshape.3
  83.7 0.0 copy-done
  83.7 0.1 reshape.283
  83.8 0.1 reduce_sum.108
  84.0 0.6 gather_fusion.1
  84.7 0.5 fusion.9
  (12 shorter events, 0.2 us)
Async XLA Ops:
  46.9 32.8 %copy-start.1 = (s32[1,4,32,1]{2,3,1,0:T(1,128)S(1)}, s32[1,4,32,1]{2,3,1,0:T(1,128)}, u32[]{:S(2)}) copy-start(s32[1,4,32,1]{2,3,1,0:T(1,128)} %param.17) | copy-start | bytes 1540
  46.9 35.3 %copy-start.2 = (f32[1,4,32]{2,1,0:T(4,128)S(1)}, f32[1,4,32]{2,1,0:T(4,128)}, u32[]{:S(2)}) copy-start(f32[1,4,32]{2,1,0:T(4,128)} %param.19) | copy-start | bytes 1540
  46.9 36.8 %copy-start = (f32[32,128]{1,0:T(8,128)S(1)}, f32[32,128]{1,0:T(8,128)}, u32[]{:S(2)}) copy-start(f32[32,128]{1,0:T(8,128)} %get-tuple-element.32) | copy-start | bytes 49156

commit v9 on v7

--- a/solution.py
+++ b/solution.py
@@ -293,17 +293,16 @@
     lanes = slots * qlen
 
     groups = lax.axis_size("blk")
-    length_row = jnp.zeros((16, dim), jnp.bfloat16).at[0, :query_count].set(
-        positive_lengths[0].astype(jnp.bfloat16)
-    )
-    id_rows = jnp.stack(
+    length_row = jnp.pad(
+        positive_lengths[0].astype(jnp.bfloat16), (0, 16 * dim - query_count)
+    ).reshape(16, dim)
+    id_rows = jnp.concatenate(
         [
             jnp.clip(owners[0, :, :, 0].reshape(pairs), 0, peer_count - 1),
             jnp.clip(local_ids[0].reshape(pairs), 0, pass_count - 1),
         ]
     ).astype(jnp.bfloat16)
-    id_rows = id_rows.reshape(2 * pairs // dim, dim)
-    id_block = jnp.zeros((16, dim), jnp.bfloat16).at[: id_rows.shape[0]].set(id_rows)
+    id_block = jnp.pad(id_rows, (0, 16 * dim - 2 * pairs)).reshape(16, dim)
     side = math.isqrt(peer_count)
     gathered, column_docs, passage_unit, raw_cross = gather_plane(
         queries[0].reshape(query_count * qlen, dim),

time: 85.3 us -> 86.1 us (level)
    another operation x3 -> x2, other arithmetic: 2 us -> 0.7 us
where the time goes in v9:
time: 86.1 us; the launch traced here: 85.7 us
  Pallas kernels  72.1 us (84%)
  other arithmetic  6.86 us (8%)
  local copies, waits for them, and re-layouts  6 us (7%)
    pallas_call x1, Pallas kernels, gather_plane(): pl.pallas_call(functools.partial(exchange_kernel, side=side, plen=plen),...  40.9 us
    pallas_call x1, Pallas kernels, score_and_return(): pl.pallas_call(functools.partial(score_return_kernel, side=side), out_sha...  31.2 us

profile of v9, /device:TPU:6, one launch (start us, length us, event | category | flops | bytes accessed | tf_op | source)
XLA Modules:
  0.0 85.7 jit_solution(16179064549418838820)
XLA Ops:
  0.6 0.7 convert_bitcast_fusion.1
  1.3 0.8 fusion.5
  2.2 0.7 clamp_convert_fusion
  2.8 0.1 min.43
  2.9 0.7 broadcast_clamp_fusion
  3.6 0.1 min.44
  3.7 0.1 min.40
  3.8 0.6 fusion.4
  4.4 0.1 fusion
  4.5 0.2 reduce_window_sum.23
  4.7 0.2 select_reduce_fusion
  4.9 40.9 %shard_map.103 = (bf16[64,144,128]{2,1,0:T(8,128)(2,1)}, bf16[8,784,128]{2,1,0:T(8,128)(2,1)}, bf16[16,192,128]{2,1,0:T(8,128)(2,1)}, f32[32,128]{1,0:T(8,128)}) custom-call(bf16[128,128]{1,0:T(8,128)(2,1)} %bitcast.51, bf16[16,128]{1,0:T(8,128)(2,1)} %get-tuple-element.19.id_ref, bf16[768,128]{1,0:T(8,128)(2,1)} %bitcast.48, ...), custom_call_target="tpu_custom_call" | custom-call | tf_op jit(solution)/shard_map/pallas_call | solution.py:162
  45.8 0.8 reshape.215
  46.6 0.1 reduce_sum.108
  46.7 0.6 gather_fusion.1
  47.4 0.5 fusion.10
  47.9 0.9 %slice_convert_fusion = s32[64,2,128]{2,1,0:T(2,128)S(1)} fusion(bf16[64,144,128]{2,1,0:T(8,128)(2,1)} %get-tuple-element.6.g_ref), kind=kLoop, calls=%fused_computation.11 | loop fusion | flops 16384 | bytes 98304 | tf_op jit(solution)/shard_map/convert_element_type | solution.py:324
  48.8 0.1 fusion.17
  48.9 0.3 reduce_window_sum.22
  49.2 0.2 select_reduce_fusion.4
  49.4 0.1 copy.20
  49.5 0.7 reshape.212.pid_ref
  50.1 0.0 copy-start
  50.1 31.2 %shard_map.104 = f32[64,8,128]{2,1,0:T(8,128)} custom-call(s32[256]{0:T(256)} %reshape.212.pid_ref, s32[16]{0:T(128)} %bitcast.58, bf16[64,144,128]{2,1,0:T(8,128)(2,1)} %get-tuple-element.6.g_ref, bf16[16,192,128]{2,1,0:T(8,128)(2,1)} %get-tuple-element.7.p_ref), custom_call_target="tpu_custom_call" | custom-call | flops 1610612736 | bytes 3145728 | tf_op jit(solution)/shard_map/pallas_call | solution.py:262
  81.3 1.0 %slice.15 = f32[64,4,128]{2,1,0:T(4,128)S(1)} slice(f32[64,8,128]{2,1,0:T(8,128)} %shard_map.104), slice={[0:64], [0:4], [0:128]} | slice | bytes 262144 | tf_op jit(solution)/shard_map/slice | solution.py:334
  82.3 0.1 copy.21
  82.5 1.6 %gather_fusion = f32[128]{0:T(128)S(1)} fusion(f32[64,4,4]{0,2,1:T(4,128)S(1)} %bitcast_reduce_fusion, s32[128]{0:T(128)S(1)} %fusion.9), kind=kCustom, calls=%fused_computation | custom fusion | bytes 2560 | tf_op jit(solution)/shard_map/gather | solution.py:343
  84.1 0.1 reshape.214
  84.2 0.1 exponential_reduce_fusion.1
  84.3 0.0 copy-done
  84.3 0.7 multiply_reduce_fusion
  85.0 0.7 broadcast_in_dim_reshape.3
  (12 shorter events, 0.2 us)
Async XLA Ops:
  50.1 34.2 %copy-start = (f32[1,4,32]{2,1,0:T(4,128)S(1)}, f32[1,4,32]{2,1,0:T(4,128)}, u32[]{:S(2)}) copy-start(f32[1,4,32]{2,1,0:T(4,128)} %param.15) | copy-start | bytes 1540

commit v10 on v7

--- a/solution.py
+++ b/solution.py
@@ -220,14 +220,13 @@
             x_buf[s, pl.ds(r, 1), :] = jnp.max(sim, axis=0, keepdims=True)
         return carry
 
-    lax.fori_loop(0, count, body, 0)
-    pl.semaphore_wait(barrier, count - 1)
-
     def slot_of(t):
         return odd * ((t % side) * side + t // side) + (1 - odd) * t
 
+    def source_of(s):
+        return odd * ((s % side) * side + s // side) + (1 - odd) * s
+
     own = pltpu.make_async_copy(x_buf.at[slot_of(me)], o_ref.at[me], own_sem)
-    own.start()
 
     def describe(d):
         target = (me + d) % count
@@ -240,9 +239,32 @@
             device_id_type=mesh_ids,
         )
 
-    def start(d, carry):
-        describe(d).start()
-        return carry
+    def send(s):
+        d = (source_of(s) + count - me) % count
+
+        @pl.when(d == 0)
+        def _():
+            own.start()
+
+        @pl.when(d != 0)
+        def _():
+            describe(d).start()
+
+    def send_one(s, carry):
+        send(s)
+        return carry
+
+    def score_then_send(s, carry):
+        body(s, carry)
+        send(s - 1)
+        return carry
+
+    early = count // 4
+    lax.fori_loop(0, early, body, 0)
+    pl.semaphore_wait(barrier, count - 1)
+    lax.fori_loop(0, early - 1, send_one, 0)
+    lax.fori_loop(early, count, score_then_send, 0)
+    send(count - 1)
 
     def finish(d, carry):
         copy = describe(d)
@@ -250,7 +272,6 @@
         copy.wait_send()
         return carry
 
-    lax.fori_loop(1, count, start, 0)
     own.wait()
     lax.fori_loop(1, count, finish, 0)
 

time: 85.3 us -> 80.7 us (0.946)
  the two profiles are of different devices: /device:TPU:6 before, /device:TPU:58 now
where the time goes in v10:
time: 80.7 us; the launch traced here: 80.4 us
  Pallas kernels  67.4 us (84%)
  other arithmetic  6.2 us (8%)
  local copies, waits for them, and re-layouts  5.97 us (7%)
    pallas_call x1, Pallas kernels, gather_plane(): pl.pallas_call(functools.partial(exchange_kernel, side=side, plen=plen),...  38.2 us
    pallas_call x1, Pallas kernels, score_and_return(): pl.pallas_call(functools.partial(score_return_kernel, side=side), out_sha...  29.2 us
    gather x1, local copies, waits for them, and re-layouts, per_device(): per_query[my_owner, jnp.minimum(my_rank, slots - 1), my_query]  1.62 us

profile of v10, /device:TPU:58, one launch (start us, length us, event | category | flops | bytes accessed | tf_op | source)
XLA Modules:
  0.0 80.4 jit_solution(4917467047303931973)
XLA Ops:
  0.6 0.7 convert_reduce_fusion
  1.3 0.1 min.42
  1.4 0.7 clamp_convert_fusion
  2.1 0.1 min.45
  2.2 0.6 fusion.3.id_ref
  2.8 0.7 convert_element_type.17
  3.5 0.6 scatter.9.lrow_ref
  4.1 38.2 %shard_map.103 = (bf16[64,144,128]{2,1,0:T(8,128)(2,1)}, bf16[8,784,128]{2,1,0:T(8,128)(2,1)}, bf16[16,192,128]{2,1,0:T(8,128)(2,1)}, f32[32,128]{1,0:T(8,128)}) custom-call(bf16[128,128]{1,0:T(8,128)(2,1)} %bitcast.45, bf16[16,128]{1,0:T(8,128)(2,1)} %fusion.3.id_ref, bf16[768,128]{1,0:T(8,128)(2,1)} %bitcast.42, bf16[16,128]{1,0:T(8,128)(2,1)} %scatter.9.lrow_ref, ...), custom_call_target="tpu_custom_call" | custom-call | tf_op jit(solution)/shard_map/pallas_call | solution.py:162
  42.3 0.9 %slice_convert_fusion = s32[64,2,128]{2,1,0:T(2,128)S(1)} fusion(bf16[64,144,128]{2,1,0:T(8,128)(2,1)} %get-tuple-element.30.g_ref), kind=kLoop, calls=%fused_computation.11 | loop fusion | flops 16384 | bytes 98304 | tf_op jit(solution)/shard_map/convert_element_type | solution.py:346
  43.2 0.1 fusion.16
  43.3 0.3 reduce_window_sum.22
  43.6 0.2 select_reduce_fusion.4
  43.8 0.1 copy.20
  43.9 0.7 reshape.280.pid_ref
  44.6 0.0 copy-start.1
  44.6 0.0 copy-start.2
  44.6 0.0 copy-start
  44.6 29.2 %shard_map.104 = f32[64,8,128]{2,1,0:T(8,128)} custom-call(s32[256]{0:T(256)} %reshape.280.pid_ref, s32[16]{0:T(128)} %bitcast.52, bf16[64,144,128]{2,1,0:T(8,128)(2,1)} %get-tuple-element.30.g_ref, bf16[16,192,128]{2,1,0:T(8,128)(2,1)} %get-tuple-element.31.p_ref), custom_call_target="tpu_custom_call" | custom-call | flops 1610612736 | bytes 3145728 | tf_op jit(solution)/shard_map/pallas_call | solution.py:283
  73.8 1.0 %slice.47 = f32[64,4,128]{2,1,0:T(4,128)S(1)} slice(f32[64,8,128]{2,1,0:T(8,128)} %shard_map.104), slice={[0:64], [0:4], [0:128]} | slice | bytes 262144 | tf_op jit(solution)/shard_map/slice | solution.py:356
  74.7 0.1 copy.21
  74.9 0.0 copy-done.1
  75.0 0.1 min.47
  75.0 0.1 fusion
  75.1 0.2 reduce_window_sum.23
  75.3 0.2 select_reduce_fusion
  75.5 0.1 min.46
  75.6 1.6 %gather_fusion = f32[128]{0:T(128)S(1)} fusion(f32[64,4,4]{0,2,1:T(4,128)S(1)} %bitcast_reduce_fusion, s32[128]{0:T(128)S(1)} %fusion.8), kind=kCustom, calls=%fused_computation | custom fusion | bytes 2560 | tf_op jit(solution)/shard_map/gather | solution.py:365
  77.2 0.1 reshape.282
  77.3 0.1 exponential_reduce_fusion.1
  77.4 0.0 copy-done.2
  77.4 0.1 fusion.4
  77.6 0.7 multiply_reduce_fusion
  78.3 0.7 broadcast_in_dim_reshape.3
  78.9 0.0 copy-done
  79.0 0.1 reshape.283
  79.0 0.1 reduce_sum.108
  79.2 0.6 gather_fusion.1
  79.9 0.5 fusion.9
  (12 shorter events, 0.2 us)
Async XLA Ops:
  44.6 30.4 %copy-start.1 = (s32[1,4,32,1]{2,3,1,0:T(1,128)S(1)}, s32[1,4,32,1]{2,3,1,0:T(1,128)}, u32[]{:S(2)}) copy-start(s32[1,4,32,1]{2,3,1,0:T(1,128)} %param.17) | copy-start | bytes 1540
  44.6 32.9 %copy-start.2 = (f32[1,4,32]{2,1,0:T(4,128)S(1)}, f32[1,4,32]{2,1,0:T(4,128)}, u32[]{:S(2)}) copy-start(f32[1,4,32]{2,1,0:T(4,128)} %param.19) | copy-start | bytes 1540
  44.6 34.4 %copy-start = (f32[32,128]{1,0:T(8,128)S(1)}, f32[32,128]{1,0:T(8,128)}, u32[]{:S(2)}) copy-start(f32[32,128]{1,0:T(8,128)} %get-tuple-element.32) | copy-start | bytes 49156

commit v11 on v10

--- a/solution.py
+++ b/solution.py
@@ -208,6 +208,7 @@
     lax.fori_loop(1, count, signal, 0)
     x_buf[...] = jnp.zeros(x_buf.shape, jnp.float32)
     row_ids = lax.broadcasted_iota(jnp.int32, (plen, lanes), 0)
+    always = lanes // slots
 
     def body(s, carry):
         q = g_ref[s, 0:lanes, :]
@@ -216,8 +217,10 @@
             sim = lax.dot_general(
                 p_ref[pidx], q, (((1,), (1,)), ((), ())), preferred_element_type=jnp.float32
             )
-            sim = jnp.where(row_ids < len_ref[pidx], sim, NEG)
-            x_buf[s, pl.ds(r, 1), :] = jnp.max(sim, axis=0, keepdims=True)
+            tail = jnp.where(row_ids[always:] < len_ref[pidx], sim[always:], NEG)
+            x_buf[s, pl.ds(r, 1), :] = jnp.maximum(
+                jnp.max(sim[:always], axis=0, keepdims=True), jnp.max(tail, axis=0, keepdims=True)
+            )
         return carry
 
     def slot_of(t):

time: 80.7 us -> 80.8 us (level)
  no operation moved by 1% of the time
where the time goes in v11:
time: 80.8 us; the launch traced here: 80.5 us
  Pallas kernels  67.5 us (84%)
  other arithmetic  6.2 us (8%)
  local copies, waits for them, and re-layouts  5.97 us (7%)
    pallas_call x1, Pallas kernels, gather_plane(): pl.pallas_call(functools.partial(exchange_kernel, side=side, plen=plen),...  38.2 us
    pallas_call x1, Pallas kernels, score_and_return(): pl.pallas_call(functools.partial(score_return_kernel, side=side), out_sha...  29.3 us
    gather x1, local copies, waits for them, and re-layouts, per_device(): per_query[my_owner, jnp.minimum(my_rank, slots - 1), my_query]  1.62 us

profile of v11, /device:TPU:58, one launch (start us, length us, event | category | flops | bytes accessed | tf_op | source)
XLA Modules:
  0.0 80.5 jit_solution(3952427607113396658)
XLA Ops:
  0.6 0.7 convert_reduce_fusion
  1.3 0.1 min.42
  1.4 0.7 clamp_convert_fusion
  2.1 0.1 min.45
  2.2 0.6 fusion.3.id_ref
  2.8 0.7 convert_element_type.17
  3.5 0.6 scatter.9.lrow_ref
  4.1 38.2 %shard_map.103 = (bf16[64,144,128]{2,1,0:T(8,128)(2,1)}, bf16[8,784,128]{2,1,0:T(8,128)(2,1)}, bf16[16,192,128]{2,1,0:T(8,128)(2,1)}, f32[32,128]{1,0:T(8,128)}) custom-call(bf16[128,128]{1,0:T(8,128)(2,1)} %bitcast.45, bf16[16,128]{1,0:T(8,128)(2,1)} %fusion.3.id_ref, bf16[768,128]{1,0:T(8,128)(2,1)} %bitcast.42, bf16[16,128]{1,0:T(8,128)(2,1)} %scatter.9.lrow_ref, ...), custom_call_target="tpu_custom_call" | custom-call | tf_op jit(solution)/shard_map/pallas_call | solution.py:162
  42.3 0.9 %slice_convert_fusion = s32[64,2,128]{2,1,0:T(2,128)S(1)} fusion(bf16[64,144,128]{2,1,0:T(8,128)(2,1)} %get-tuple-element.30.g_ref), kind=kLoop, calls=%fused_computation.11 | loop fusion | flops 16384 | bytes 98304 | tf_op jit(solution)/shard_map/convert_element_type | solution.py:349
  43.2 0.1 fusion.16
  43.3 0.3 reduce_window_sum.22
  43.6 0.2 select_reduce_fusion.4
  43.8 0.1 copy.20
  43.9 0.7 reshape.280.pid_ref
  44.6 0.0 copy-start.1
  44.6 0.0 copy-start.2
  44.6 0.0 copy-start
  44.6 29.3 %shard_map.104 = f32[64,8,128]{2,1,0:T(8,128)} custom-call(s32[256]{0:T(256)} %reshape.280.pid_ref, s32[16]{0:T(128)} %bitcast.52, bf16[64,144,128]{2,1,0:T(8,128)(2,1)} %get-tuple-element.30.g_ref, bf16[16,192,128]{2,1,0:T(8,128)(2,1)} %get-tuple-element.31.p_ref), custom_call_target="tpu_custom_call" | custom-call | flops 1610612736 | bytes 3145728 | tf_op jit(solution)/shard_map/pallas_call | solution.py:286
  73.9 1.0 %slice.47 = f32[64,4,128]{2,1,0:T(4,128)S(1)} slice(f32[64,8,128]{2,1,0:T(8,128)} %shard_map.104), slice={[0:64], [0:4], [0:128]} | slice | bytes 262144 | tf_op jit(solution)/shard_map/slice | solution.py:359
  74.8 0.1 copy.21
  75.0 0.0 copy-done.1
  75.0 0.1 min.47
  75.1 0.1 fusion
  75.2 0.2 reduce_window_sum.23
  75.4 0.2 select_reduce_fusion
  75.6 0.1 min.46
  75.7 1.6 %gather_fusion = f32[128]{0:T(128)S(1)} fusion(f32[64,4,4]{0,2,1:T(4,128)S(1)} %bitcast_reduce_fusion, s32[128]{0:T(128)S(1)} %fusion.8), kind=kCustom, calls=%fused_computation | custom fusion | bytes 2560 | tf_op jit(solution)/shard_map/gather | solution.py:368
  77.3 0.1 reshape.282
  77.4 0.1 exponential_reduce_fusion.1
  77.5 0.0 copy-done.2
  77.5 0.1 fusion.4
  77.7 0.7 multiply_reduce_fusion
  78.4 0.7 broadcast_in_dim_reshape.3
  79.0 0.0 copy-done
  79.0 0.1 reshape.283
  79.1 0.1 reduce_sum.108
  79.3 0.6 gather_fusion.1
  80.0 0.5 fusion.9
  (12 shorter events, 0.2 us)
Async XLA Ops:
  44.6 30.5 %copy-start.1 = (s32[1,4,32,1]{2,3,1,0:T(1,128)S(1)}, s32[1,4,32,1]{2,3,1,0:T(1,128)}, u32[]{:S(2)}) copy-start(s32[1,4,32,1]{2,3,1,0:T(1,128)} %param.17) | copy-start | bytes 1540
  44.6 33.0 %copy-start.2 = (f32[1,4,32]{2,1,0:T(4,128)S(1)}, f32[1,4,32]{2,1,0:T(4,128)}, u32[]{:S(2)}) copy-start(f32[1,4,32]{2,1,0:T(4,128)} %param.19) | copy-start | bytes 1540
  44.6 34.5 %copy-start = (f32[32,128]{1,0:T(8,128)S(1)}, f32[32,128]{1,0:T(8,128)}, u32[]{:S(2)}) copy-start(f32[32,128]{1,0:T(8,128)} %get-tuple-element.32) | copy-start | bytes 49156

commit v12 on v10

--- a/solution.py
+++ b/solution.py
@@ -259,7 +259,7 @@
         send(s - 1)
         return carry
 
-    early = count // 4
+    early = count // 8
     lax.fori_loop(0, early, body, 0)
     pl.semaphore_wait(barrier, count - 1)
     lax.fori_loop(0, early - 1, send_one, 0)

time: 80.7 us -> 82.6 us (1.024)
  Pallas kernels: 67.4 us -> 69.3 us
    pallas_call x1, Pallas kernels: 29.2 us -> 31.1 us  [score_and_return(): pl.pallas_call(functools.partial(score_return_kernel, side=side), out_sha...]
where the time goes in v12:
time: 82.6 us; the launch traced here: 82.3 us
  Pallas kernels  69.3 us (84%)
  other arithmetic  6.2 us (8%)
  local copies, waits for them, and re-layouts  5.97 us (7%)
    pallas_call x1, Pallas kernels, gather_plane(): pl.pallas_call(functools.partial(exchange_kernel, side=side, plen=plen),...  38.2 us
    pallas_call x1, Pallas kernels, score_and_return(): pl.pallas_call(functools.partial(score_return_kernel, side=side), out_sha...  31.1 us

profile of v12, /device:TPU:58, one launch (start us, length us, event | category | flops | bytes accessed | tf_op | source)
XLA Modules:
  0.0 82.3 jit_solution(175482038437126209)
XLA Ops:
  0.6 0.7 convert_reduce_fusion
  1.3 0.1 min.42
  1.4 0.7 clamp_convert_fusion
  2.1 0.1 min.45
  2.2 0.6 fusion.3.id_ref
  2.8 0.7 convert_element_type.17
  3.5 0.6 scatter.9.lrow_ref
  4.1 38.2 %shard_map.103 = (bf16[64,144,128]{2,1,0:T(8,128)(2,1)}, bf16[8,784,128]{2,1,0:T(8,128)(2,1)}, bf16[16,192,128]{2,1,0:T(8,128)(2,1)}, f32[32,128]{1,0:T(8,128)}) custom-call(bf16[128,128]{1,0:T(8,128)(2,1)} %bitcast.45, bf16[16,128]{1,0:T(8,128)(2,1)} %fusion.3.id_ref, bf16[768,128]{1,0:T(8,128)(2,1)} %bitcast.42, bf16[16,128]{1,0:T(8,128)(2,1)} %scatter.9.lrow_ref, ...), custom_call_target="tpu_custom_call" | custom-call | tf_op jit(solution)/shard_map/pallas_call | solution.py:162
  42.3 0.9 %slice_convert_fusion = s32[64,2,128]{2,1,0:T(2,128)S(1)} fusion(bf16[64,144,128]{2,1,0:T(8,128)(2,1)} %get-tuple-element.30.g_ref), kind=kLoop, calls=%fused_computation.11 | loop fusion | flops 16384 | bytes 98304 | tf_op jit(solution)/shard_map/convert_element_type | solution.py:346
  43.2 0.1 fusion.16
  43.3 0.3 reduce_window_sum.22
  43.6 0.2 select_reduce_fusion.4
  43.8 0.1 copy.20
  43.9 0.7 reshape.280.pid_ref
  44.6 0.0 copy-start.1
  44.6 0.0 copy-start.2
  44.6 0.0 copy-start
  44.6 31.1 %shard_map.104 = f32[64,8,128]{2,1,0:T(8,128)} custom-call(s32[256]{0:T(256)} %reshape.280.pid_ref, s32[16]{0:T(128)} %bitcast.52, bf16[64,144,128]{2,1,0:T(8,128)(2,1)} %get-tuple-element.30.g_ref, bf16[16,192,128]{2,1,0:T(8,128)(2,1)} %get-tuple-element.31.p_ref), custom_call_target="tpu_custom_call" | custom-call | flops 1610612736 | bytes 3145728 | tf_op jit(solution)/shard_map/pallas_call | solution.py:283
  75.6 1.0 %slice.47 = f32[64,4,128]{2,1,0:T(4,128)S(1)} slice(f32[64,8,128]{2,1,0:T(8,128)} %shard_map.104), slice={[0:64], [0:4], [0:128]} | slice | bytes 262144 | tf_op jit(solution)/shard_map/slice | solution.py:356
  76.6 0.1 copy.21
  76.8 0.0 copy-done.1
  76.8 0.1 min.47
  76.9 0.1 fusion
  77.0 0.2 reduce_window_sum.23
  77.2 0.2 select_reduce_fusion
  77.3 0.1 min.46
  77.5 1.6 %gather_fusion = f32[128]{0:T(128)S(1)} fusion(f32[64,4,4]{0,2,1:T(4,128)S(1)} %bitcast_reduce_fusion, s32[128]{0:T(128)S(1)} %fusion.8), kind=kCustom, calls=%fused_computation | custom fusion | bytes 2560 | tf_op jit(solution)/shard_map/gather | solution.py:365
  79.1 0.1 reshape.282
  79.2 0.1 exponential_reduce_fusion.1
  79.3 0.0 copy-done.2
  79.3 0.1 fusion.4
  79.4 0.7 multiply_reduce_fusion
  80.2 0.7 broadcast_in_dim_reshape.3
  80.8 0.0 copy-done
  80.8 0.1 reshape.283
  80.9 0.1 reduce_sum.108
  81.1 0.6 gather_fusion.1
  81.7 0.5 fusion.9
  (12 shorter events, 0.2 us)
Async XLA Ops:
  44.6 32.2 %copy-start.1 = (s32[1,4,32,1]{2,3,1,0:T(1,128)S(1)}, s32[1,4,32,1]{2,3,1,0:T(1,128)}, u32[]{:S(2)}) copy-start(s32[1,4,32,1]{2,3,1,0:T(1,128)} %param.17) | copy-start | bytes 1540
  44.6 34.7 %copy-start.2 = (f32[1,4,32]{2,1,0:T(4,128)S(1)}, f32[1,4,32]{2,1,0:T(4,128)}, u32[]{:S(2)}) copy-start(f32[1,4,32]{2,1,0:T(4,128)} %param.19) | copy-start | bytes 1540
  44.6 36.2 %copy-start = (f32[32,128]{1,0:T(8,128)S(1)}, f32[32,128]{1,0:T(8,128)}, u32[]{:S(2)}) copy-start(f32[32,128]{1,0:T(8,128)} %get-tuple-element.32) | copy-start | bytes 49156

commit v13 on v12

--- a/solution.py
+++ b/solution.py
@@ -259,7 +259,7 @@
         send(s - 1)
         return carry
 
-    early = count // 8
+    early = count * 3 // 8
     lax.fori_loop(0, early, body, 0)
     pl.semaphore_wait(barrier, count - 1)
     lax.fori_loop(0, early - 1, send_one, 0)

time: 82.6 us -> 80.7 us (0.977)
  the two profiles are of different devices: /device:TPU:58 before, /device:TPU:62 now
where the time goes in v13:
time: 80.7 us; the launch traced here: 80.4 us
  Pallas kernels  67.4 us (84%)
  other arithmetic  6.2 us (8%)
  local copies, waits for them, and re-layouts  5.97 us (7%)
    pallas_call x1, Pallas kernels, gather_plane(): pl.pallas_call(functools.partial(exchange_kernel, side=side, plen=plen),...  38.2 us
    pallas_call x1, Pallas kernels, score_and_return(): pl.pallas_call(functools.partial(score_return_kernel, side=side), out_sha...  29.2 us
    gather x1, local copies, waits for them, and re-layouts, per_device(): per_query[my_owner, jnp.minimum(my_rank, slots - 1), my_query]  1.62 us

profile of v13, /device:TPU:62, one launch (start us, length us, event | category | flops | bytes accessed | tf_op | source)
XLA Modules:
  0.0 80.4 jit_solution(16987348491447205848)
XLA Ops:
  0.6 0.7 convert_reduce_fusion
  1.3 0.1 min.42
  1.4 0.7 clamp_convert_fusion
  2.1 0.1 min.45
  2.2 0.6 fusion.3.id_ref
  2.8 0.7 convert_element_type.17
  3.5 0.6 scatter.9.lrow_ref
  4.1 38.2 %shard_map.103 = (bf16[64,144,128]{2,1,0:T(8,128)(2,1)}, bf16[8,784,128]{2,1,0:T(8,128)(2,1)}, bf16[16,192,128]{2,1,0:T(8,128)(2,1)}, f32[32,128]{1,0:T(8,128)}) custom-call(bf16[128,128]{1,0:T(8,128)(2,1)} %bitcast.45, bf16[16,128]{1,0:T(8,128)(2,1)} %fusion.3.id_ref, bf16[768,128]{1,0:T(8,128)(2,1)} %bitcast.42, bf16[16,128]{1,0:T(8,128)(2,1)} %scatter.9.lrow_ref, ...), custom_call_target="tpu_custom_call" | custom-call | tf_op jit(solution)/shard_map/pallas_call | solution.py:162
  42.3 0.9 %slice_convert_fusion = s32[64,2,128]{2,1,0:T(2,128)S(1)} fusion(bf16[64,144,128]{2,1,0:T(8,128)(2,1)} %get-tuple-element.30.g_ref), kind=kLoop, calls=%fused_computation.11 | loop fusion | flops 16384 | bytes 98304 | tf_op jit(solution)/shard_map/convert_element_type | solution.py:346
  43.2 0.1 fusion.16
  43.3 0.3 reduce_window_sum.22
  43.6 0.2 select_reduce_fusion.4
  43.8 0.1 copy.20
  43.9 0.7 reshape.280.pid_ref
  44.6 0.0 copy-start.1
  44.6 0.0 copy-start.2
  44.6 0.0 copy-start
  44.6 29.2 %shard_map.104 = f32[64,8,128]{2,1,0:T(8,128)} custom-call(s32[256]{0:T(256)} %reshape.280.pid_ref, s32[16]{0:T(128)} %bitcast.52, bf16[64,144,128]{2,1,0:T(8,128)(2,1)} %get-tuple-element.30.g_ref, bf16[16,192,128]{2,1,0:T(8,128)(2,1)} %get-tuple-element.31.p_ref), custom_call_target="tpu_custom_call" | custom-call | flops 1610612736 | bytes 3145728 | tf_op jit(solution)/shard_map/pallas_call | solution.py:283
  73.8 1.0 %slice.47 = f32[64,4,128]{2,1,0:T(4,128)S(1)} slice(f32[64,8,128]{2,1,0:T(8,128)} %shard_map.104), slice={[0:64], [0:4], [0:128]} | slice | bytes 262144 | tf_op jit(solution)/shard_map/slice | solution.py:356
  74.7 0.1 copy.21
  74.9 0.0 copy-done.1
  74.9 0.1 min.47
  75.0 0.1 fusion
  75.1 0.2 reduce_window_sum.23
  75.3 0.2 select_reduce_fusion
  75.5 0.1 min.46
  75.6 1.6 %gather_fusion = f32[128]{0:T(128)S(1)} fusion(f32[64,4,4]{0,2,1:T(4,128)S(1)} %bitcast_reduce_fusion, s32[128]{0:T(128)S(1)} %fusion.8), kind=kCustom, calls=%fused_computation | custom fusion | bytes 2560 | tf_op jit(solution)/shard_map/gather | solution.py:365
  77.2 0.1 reshape.282
  77.3 0.1 exponential_reduce_fusion.1
  77.4 0.0 copy-done.2
  77.4 0.1 fusion.4
  77.6 0.7 multiply_reduce_fusion
  78.3 0.7 broadcast_in_dim_reshape.3
  78.9 0.0 copy-done
  78.9 0.1 reshape.283
  79.0 0.1 reduce_sum.108
  79.2 0.6 gather_fusion.1
  79.9 0.5 fusion.9
  (12 shorter events, 0.2 us)
Async XLA Ops:
  44.6 30.3 %copy-start.1 = (s32[1,4,32,1]{2,3,1,0:T(1,128)S(1)}, s32[1,4,32,1]{2,3,1,0:T(1,128)}, u32[]{:S(2)}) copy-start(s32[1,4,32,1]{2,3,1,0:T(1,128)} %param.17) | copy-start | bytes 1540
  44.6 32.9 %copy-start.2 = (f32[1,4,32]{2,1,0:T(4,128)S(1)}, f32[1,4,32]{2,1,0:T(4,128)}, u32[]{:S(2)}) copy-start(f32[1,4,32]{2,1,0:T(4,128)} %param.19) | copy-start | bytes 1540
  44.6 34.4 %copy-start = (f32[32,128]{1,0:T(8,128)S(1)}, f32[32,128]{1,0:T(8,128)}, u32[]{:S(2)}) copy-start(f32[32,128]{1,0:T(8,128)} %get-tuple-element.32) | copy-start | bytes 49156
